TPU v7x, 256 devices: a whole 4x4x8 slice. The times are simulated.
256 devices in a mesh: expert: 32 (over x, z), tensor: 8 (over y, core).
Axes of the slice: x: 4, y: 4, z: 8, core: 2. Of those that a mesh axis runs over, the one named last changes fastest.
Arguments:
- tokens: bfloat16 [8192, 4096], P('expert'), may hold values from -6 to 6
- cotangent: bfloat16 [8192, 4096], P('expert'), may hold values from -1.5 to 1.5
- w_in: bfloat16 [4096, 65536], P(None, ('expert', 'tensor')), may hold values from -0.09375 to 0.09375
- w_out: bfloat16 [65536, 4096], P(('expert', 'tensor')), may hold values from -0.09375 to 0.09375
- router: bfloat16 [4096, 16], replicated, may hold values from -0.09375 to 0.09375
- chosen: int32 [16, 512], replicated, may hold values from 0 to 8191, as said below
Outputs:
- grad_tokens: bfloat16 [8192, 4096], P('expert', 'tensor')
- grad_in: bfloat16 [4096, 65536], P(None, ('expert', 'tensor'))
- grad_out: bfloat16 [65536, 4096], P(('expert', 'tensor'))
- grad_router: float32 [4096, 16], replicated
Inputs may be any that keep to these rules, and one draw needn't show every extreme that they name: Row e lists, in increasing order, 512 distinct tokens chosen by expert e; at most 32 of them lie among one device's 256 consecutive tokens, and in every row some device's tokens hold exactly 32 of them.
All inputs are finite; a program needn't handle non-finite values.
Results may differ from a plain program's by a relative error of at most 0.005.
Values may be sent and summed in bfloat16 or wider, within the bound.
A program may use at most 128 MiB of HBM per device.

v0:
```python
import jax
import jax.numpy as jnp
from jax import lax
from jax.sharding import PartitionSpec as P


def body(tokens, cotangent, w_in, w_out, router, chosen):
    tok_dev, features = tokens.shape
    n_expert = lax.axis_size("expert")
    bucket = 4 * tok_dev // n_expert
    capacity = chosen.shape[1]
    expert_total = router.shape[1]
    device_index = lax.axis_index("expert")
    expert = device_index // 2
    slot_range = jnp.arange(bucket, dtype=jnp.int32)
    first_token = device_index * tok_dev
    starts = jnp.sum((chosen < first_token).astype(jnp.int32), axis=1)
    run_ends = jnp.sum((chosen < first_token + tok_dev).astype(jnp.int32), axis=1)
    counts = run_ends - starts
    positions = jnp.minimum(starts[:, None] + slot_range[None, :], capacity - 1)
    picked = jnp.take_along_axis(chosen, positions, axis=1) - first_token
    filled = slot_range[None, :] < counts[:, None]
    local_rows = jnp.where(filled, picked, 0)
    owner_expert = jnp.arange(n_expert, dtype=jnp.int32) // 2
    send_rows = local_rows[owner_expert].reshape(-1)
    send_filled = filled[owner_expert].reshape(-1)

    def pack(source):
        gathered = jnp.where(send_filled[:, None], source[send_rows], jnp.zeros((), source.dtype))
        return gathered.reshape(n_expert, bucket, source.shape[1])

    got_x, got_y = (
        lax.all_to_all(pack(tokens), "expert", split_axis=0, concat_axis=0, tiled=True),
        lax.all_to_all(pack(cotangent), "expert", split_axis=0, concat_axis=0, tiled=True),
    )
    my_chosen = lax.dynamic_index_in_dim(chosen, expert, 0, keepdims=False)
    home_index = my_chosen // tok_dev
    bounds = jnp.arange(n_expert, dtype=jnp.int32) * tok_dev
    run_start = jnp.sum((my_chosen[None, :] < bounds[:, None]).astype(jnp.int32), axis=1)
    slot_index = home_index * bucket + jnp.arange(capacity, dtype=jnp.int32) - run_start[home_index]
    x_rows = got_x.reshape(-1, features)[slot_index]
    grad_rows = got_y.reshape(-1, features)[slot_index]
    r_col = lax.dynamic_slice_in_dim(router, expert, 1, 1)
    gate = jax.nn.sigmoid(jnp.dot(x_rows, r_col, preferred_element_type=jnp.float32)[:, 0])
    pre_act = jnp.dot(x_rows, w_in, preferred_element_type=jnp.float32)
    sig_act = jax.nn.sigmoid(pre_act)
    hidden = pre_act * sig_act
    upstream = jnp.dot(grad_rows, w_out.T, preferred_element_type=jnp.float32)
    gated_hidden = (gate[:, None] * hidden).astype(jnp.bfloat16)
    gate_grad = jnp.sum(hidden * upstream, axis=1)
    pre_grad = (gate[:, None] * upstream * sig_act * (1.0 + pre_act * (1.0 - sig_act))).astype(
        jnp.bfloat16
    )
    grad_out = jnp.dot(gated_hidden.T, grad_rows, preferred_element_type=jnp.float32).astype(
        jnp.bfloat16
    )
    grad_in = jnp.dot(x_rows.T, pre_grad, preferred_element_type=jnp.float32).astype(jnp.bfloat16)
    score_grad = gate_grad * gate * (1.0 - gate)
    router_col = jnp.dot(score_grad, x_rows.astype(jnp.float32), precision=lax.Precision.HIGHEST)
    router_term = (
        router_col[:, None] * (jnp.arange(expert_total) == expert).astype(jnp.float32)[None, :]
    )
    grad_router = lax.psum(router_term, ("expert", "tensor"))
    router_rows = r_col.astype(jnp.float32)
    summed = lax.psum_scatter(
        jnp.dot(w_in, pre_grad.T, preferred_element_type=jnp.float32)
        + router_rows * score_grad[None, :],
        "tensor",
        scatter_dimension=0,
        tiled=True,
    )
    share = summed.shape[0]
    outgoing = jnp.zeros((share, n_expert * bucket), jnp.float32).at[:, slot_index].set(summed)
    returned = lax.all_to_all(
        outgoing.reshape(share, n_expert, bucket), "expert", split_axis=1, concat_axis=1, tiled=True
    )
    returned = jnp.where(send_filled[None, :], returned.reshape(share, -1), 0.0)
    combined = jnp.zeros((share, tok_dev), jnp.float32).at[:, send_rows].add(returned)
    grad_tokens = combined.T.astype(jnp.bfloat16)
    return (grad_tokens, grad_in, grad_out, grad_router)


def solution(mesh):
    placed = (
        P("expert", None),
        P("expert", None),
        P(None, ("expert", "tensor")),
        P(("expert", "tensor"), None),
        P(),
        P(),
    )
    return jax.shard_map(
        body,
        mesh=mesh,
        in_specs=placed,
        out_specs=(
            P("expert", "tensor"),
            P(None, ("expert", "tensor")),
            P(("expert", "tensor"), None),
            P(),
        ),
        check_vma=False,
    )
```

profile of v0, /device:TPU:1, one launch (start us, length us, event | category | flops | bytes accessed | tf_op | source)
XLA Modules:
  0.0 806.0 jit_solution(2339139497223671526)
XLA Ops:
  8.1 1.0 convert_reduce_fusion.2
  9.2 4.5 gather_fusion.6
  15.3 7.8 gather_fusion.4
  23.1 16.9 %gather_fusion.2 = bf16[1024,4096]{1,0:T(8,128)(2,1)} fusion(bf16[256,4096]{1,0:T(8,128)(2,1)} %param.6, s32[1024]{0:T(1024)S(1)} %broadcast_clamp_fusion), kind=kCustom, calls=%fused_computation.2 | custom fusion | bytes 16781312 | tf_op jit(solution)/shard_map/gather | solution.py:29
  40.0 9.2 %broadcast_select_fusion = (bf16[32,32,4096]{2,1,0:T(8,128)(2,1)}, bf16[32,32,4096]{2,1,0:T(8,128)(2,1)S(1)}) fusion(bf16[32,32,4096]{2,1,0:T(8,128)(2,1)} %bitcast.83, pred[32,32]{1,0:T(8,128)(4,1)S(1)} %gather_fusion.1, bf16[32,32,4096]{2,1,0:T(8,128)(2,1)} %bitcast.84), kind=kLoop, calls=%fused_computation.10 | loop fusion | flops 8388608 | bytes 33555456 | tf_op jit(solution)/shard_map/jit(_where)/select_n | solution.py:29
  49.2 193.3 %all_to_all.15 = bf16[32,32,4096]{2,1,0:T(8,128)(2,1)} all-to-all(bf16[32,32,4096]{2,1,0:T(8,128)(2,1)S(1)} %get-tuple-element.37), channel_id=1, replica_groups=mesh['expert'=32,'tensor'=8] {'expert'}, dimensions={0} | all-to-all | bytes 16777216 | tf_op jit(solution)/shard_map/all_to_all | solution.py:33
  242.5 9.0 %all-to-all-start.1 = ((bf16[32,32,4096]{2,1,0:T(8,128)(2,1)}), bf16[32,32,4096]{2,1,0:T(8,128)(2,1)}, u32[]{:S(2)}, u32[]{:S(2)}) async-start(bf16[32,32,4096]{2,1,0:T(8,128)(2,1)} %get-tuple-element.36), calls=%async_computation.1 | async-start | bytes 16777216 | tf_op jit(solution)/shard_map/all_to_all | solution.py:34
  251.6 0.9 dynamic-slice_reduce_fusion
  252.8 0.7 fusion.21
  253.5 4.3 compare_select_fusion.5
  257.8 0.7 fusion.20
  258.7 15.5 %select_select_fusion = s32[512]{0:T(512)S(1)} fusion(pred[512]{0:T(512)(128)(4,1)S(1)} %get-tuple-element.30, pred[512]{0:T(512)(128)(4,1)S(1)} %get-tuple-element.29, pred[512]{0:T(512)(128)(4,1)S(1)} %get-tuple-element.28, pred[512]{0:T(512)(128)(4,1)S(1)} %get-tuple-element.27, pred[512]{0:T(512)(128)(4,1)S(1)} %get-tuple-element.26, ...), kind=kLoop, calls=%fused_computation.88 | loop fusion | flops 12800 | bytes 16996 | tf_op jit(solution)/shard_map/gather | solution.py:40
  274.3 13.3 %gather_fusion.3 = bf16[512,4096]{1,0:T(8,128)(2,1)} fusion(bf16[1024,4096]{1,0:T(8,128)(2,1)} %bitcast.82, s32[1024]{0:T(1024)S(1)} %pad_clamp_fusion), kind=kCustom, calls=%fused_computation.3 | custom fusion | bytes 8390656 | tf_op jit(solution)/shard_map/gather | solution.py:41
  287.6 3.5 fusion.9
  291.2 1.3 fusion.22
  292.5 142.1 %all-to-all-done.1 = bf16[32,32,4096]{2,1,0:T(8,128)(2,1)} async-done(((bf16[32,32,4096]{2,1,0:T(8,128)(2,1)}), bf16[32,32,4096]{2,1,0:T(8,128)(2,1)}, u32[]{:S(2)}, u32[]{:S(2)}) %all-to-all-start.1) | async-done | bytes 8388640 | tf_op jit(solution)/shard_map/all_to_all | solution.py:34
  434.6 13.0 %gather_fusion.5 = bf16[512,4096]{1,0:T(8,128)(2,1)} fusion(bf16[1024,4096]{1,0:T(8,128)(2,1)} %bitcast.43, s32[1024]{0:T(1024)S(1)} %pad_clamp_fusion), kind=kCustom, calls=%fused_computation.5 | custom fusion | bytes 8390656 | tf_op jit(solution)/shard_map/gather | solution.py:42
  447.6 4.3 multiply_reduce_fusion
  451.9 5.1 bitcast_add_fusion
  457.0 60.2 %reduce-scatter.2.cloned.1.call-done = f32[512,512]{0,1:T(8,128)} async-done(((f32[4096,512]{0,1:T(8,128)}), f32[512,512]{0,1:T(8,128)}) %reduce-scatter.2.cloned.1.call-update) | async-done | bytes 1048592 | tf_op jit(solution)/shard_map/reduce_scatter | solution.py:65
  517.2 4.4 scatter_custom_fusion
  521.6 9.7 %all-to-all-start.2 = ((f32[512,32,32]{0,2,1:T(8,128)}), f32[512,32,32]{0,2,1:T(8,128)}, u32[]{:S(2)}, u32[]{:S(2)}) async-start(f32[512,32,32]{0,2,1:T(8,128)} %bitcast.46), calls=%async_computation.3 | async-start | bytes 4194304 | tf_op jit(solution)/shard_map/all_to_all | solution.py:74
  531.5 3.9 fusion.23
  535.4 0.8 broadcast_multiply_fusion
  536.2 5.0 convolution_convert_fusion.1
  541.2 2.6 convolution_convert_fusion
  543.8 37.1 %all-to-all-done.2 = f32[512,32,32]{0,2,1:T(8,128)} async-done(((f32[512,32,32]{0,2,1:T(8,128)}), f32[512,32,32]{0,2,1:T(8,128)}, u32[]{:S(2)}, u32[]{:S(2)}) %all-to-all-start.2) | async-done | bytes 2097184 | tf_op jit(solution)/shard_map/all_to_all | solution.py:74
  581.0 3.2 bitcast_select_fusion
  584.1 7.6 scatter_custom_fusion.1
  591.7 0.7 convert_bitcast_fusion
  592.5 204.4 %all-reduce.2.cloned.1.call-done = f32[4096,16]{0,1:T(8,128)} async-done(((f32[4096,16]{0,1:T(8,128)}), f32[4096,16]{0,1:T(8,128)}) %all-reduce.2.cloned.1.call-update) | async-done | bytes 262160 | tf_op jit(solution)/shard_map/psum | solution.py:63
  796.9 1.7 copy.11
  (40 shorter events, 2.3 us)
Async XLA Ops:
  8.0 7.3 copy-start
  8.0 1.2 copy-start.2
  242.5 192.0 %all-to-all-start.1 = ((bf16[32,32,4096]{2,1,0:T(8,128)(2,1)}), bf16[32,32,4096]{2,1,0:T(8,128)(2,1)}, u32[]{:S(2)}, u32[]{:S(2)}) async-start(bf16[32,32,4096]{2,1,0:T(8,128)(2,1)} %get-tuple-element.36), calls=%async_computation.1 | async-start | bytes 16777216 | tf_op jit(solution)/shard_map/all_to_all | solution.py:34
  251.6 265.7 %reduce-scatter.2.cloned.1.call-start = ((), (), s32[]{:S(2)}) async-start(), calls=%async_computation.4 | async-start | bytes 9437184 | tf_op jit(solution)/shard_map/reduce_scatter | solution.py:65
  274.2 16.9 %copy-start.5 = (bf16[4096,256]{1,0:T(8,128)(2,1)S(1)}, bf16[4096,256]{1,0:T(8,128)(2,1)}, u32[]{:S(2)}) copy-start(bf16[4096,256]{1,0:T(8,128)(2,1)} %param.8) | copy-start | bytes 6291460
  287.6 3.5 copy-start.3
  521.6 59.3 %all-to-all-start.2 = ((f32[512,32,32]{0,2,1:T(8,128)}), f32[512,32,32]{0,2,1:T(8,128)}, u32[]{:S(2)}, u32[]{:S(2)}) async-start(f32[512,32,32]{0,2,1:T(8,128)} %bitcast.46), calls=%async_computation.3 | async-start | bytes 4194304 | tf_op jit(solution)/shard_map/all_to_all | solution.py:74
  531.3 265.6 %all-reduce.2.cloned.1.call-start = ((), (), s32[]{:S(2)}) async-start(), calls=%async_computation.5 | async-start | bytes 524288 | tf_op jit(solution)/shard_map/psum | solution.py:63
  536.2 5.0 copy-start.4
  541.2 257.4 %copy-start.1 = (bf16[256,4096]{1,0:T(8,128)(2,1)S(1)}, bf16[256,4096]{1,0:T(8,128)(2,1)}, u32[]{:S(2)}) copy-start(bf16[256,4096]{1,0:T(8,128)(2,1)} %param.7) | copy-start | bytes 6291460
Sparse Core Ops, SparseCore 0:
  457.1 60.0 reduce-scatter.1
Sparse Core Ops, SparseCore 1:
  537.8 259.0 all-reduce.1
where the time goes:
time: 808 us; the launch traced here: 806 us
  waiting for transfers between devices  444 us (55%)
  blocking collectives  193 us (24%)
  local copies, waits for them, and re-layouts  65.6 us (8%)
  other arithmetic  43 us (5%)
  matrix products  25.8 us (3%)
  starting transfers between devices  18.8 us (2%)
  between operations  15.7 us (2%)
    psum x1, waiting for transfers between devices, body(): grad_router = lax.psum(router_term, ('expert', 'tensor'))  204 us
    all_to_all x1, blocking collectives, body(): lax.all_to_all(pack(tokens), 'expert', split_axis=0, concat_axis=0, tiled...  193 us
    all_to_all x1, waiting for transfers between devices, body(): lax.all_to_all(pack(cotangent), 'expert', split_axis=0, concat_axis=0, ti...  142 us
    reduce_scatter x1, waiting for transfers between devices, body(): lax.psum_scatter(jnp.dot(w_in, pre_grad.T, preferred_element_type=jnp.flo...  60.2 us
    all_to_all x1, waiting for transfers between devices, body(): lax.all_to_all(outgoing.reshape(share, n_expert, bucket), 'expert', split...  37.1 us
    gather x2, local copies, waits for them, and re-layouts, pack(): source[send_rows]  24.8 us
    gather x3, other arithmetic, body(): run_start[home_index]  20 us
  transfers between devices with their start and end apart: 4, of which 4 were waited for; matrix products, arithmetic and copies ran while one was open for 8% of the time, Pallas kernels for 0%

commit v1 on v0

v1 whole, which is shorter than its diff:
```python
import functools

import jax
import jax.numpy as jnp
from jax import lax
from jax.experimental import pallas as pl
from jax.experimental.pallas import tpu as pltpu
from jax.sharding import PartitionSpec as P

MESH = pl.DeviceIdType.MESH
BF = jnp.bfloat16
F32 = jnp.float32
RING = 4


def mm(a, b, dims):
    return lax.dot_general(a, b, (dims, ((), ())), preferred_element_type=F32)


def step_kernel(
    ne, nt, bucket,
    tok, cot, w_in, w_out, rrow, sel_col, sel_row, q_col, q_row,
    gt, gin, gout, gr,
    tv, w1v, w2v, sx, rx, gx, acc, gp, hg, da, dsb, rb, cb, zb, yi, yj, yk, yl, zf, fv, fb, es, er,
    ginv, goutv, rp, rq, rs1, rz, rv, rw, rxs, ry,
    ld, p1s, p1r, ags, agr, cs, cr, zzs, zzr, yis, yir, yjs, yjr, yks, ykr, yls, ylr, zfs, zfr,
    rets, retr, r1s, r1r, rzs, rzr, r2s, r2r, r3s, r3r, outs,
):
    me = lax.axis_index("expert")
    t = lax.axis_index("tensor")
    h = me % 2
    y = t // 2
    c = t % 2
    feat = tv.shape[2]
    share = feat // 2
    cap = hg.shape[0]
    groups = gx.shape[1]
    half = cap // 2
    quarter = cap // 4

    zdev = (me + 1 - 2 * h, t)
    cdev = (me, 2 * y + 1 - c)
    yn = (y + 1) % RING
    yp = (y + 3) % RING
    yo = (y + 2) % RING
    ynd = (me, 2 * yn + c)
    ypd = (me, 2 * yp + c)

    def rcopy(src, dst, ss, rs, dev):
        return pltpu.make_async_remote_copy(
            src_ref=src, dst_ref=dst, send_sem=ss, recv_sem=rs, device_id=dev, device_id_type=MESH
        )

    pending = []

    def send(src, dst, ss, rs, dev):
        copy = rcopy(src, dst, ss, rs, dev)
        copy.start()
        pending.append(copy)

    def arrived(dst, rs):
        rcopy(dst, dst, rs, rs, zdev).wait_recv()

    loads = [
        pltpu.make_async_copy(tok.at[:, pl.ds(pl.multiple_of(t * feat, feat), feat)], tv.at[0], ld.at[0]),
        pltpu.make_async_copy(cot.at[:, pl.ds(pl.multiple_of(t * feat, feat), feat)], tv.at[1], ld.at[1]),
        pltpu.make_async_copy(w_in, w1v, ld.at[2]),
        pltpu.make_async_copy(w_out, w2v, ld.at[3]),
    ]
    for load in loads:
        load.start()

    barrier = pltpu.get_barrier_semaphore()

    @pl.loop(1, ne)
    def _(d):
        pl.semaphore_signal(barrier, inc=1, device_id=((me + d) % ne, t), device_id_type=MESH)

    @pl.loop(1, nt)
    def _(d):
        pl.semaphore_signal(barrier, inc=1, device_id=(me, (t + d) % nt), device_id_type=MESH)

    slots = sel_col.shape[0]
    hot = (lax.broadcasted_iota(jnp.int32, (slots, tv.shape[1]), 1) == sel_col[...]).astype(BF)

    for a in range(2):
        loads[a].wait()
        for k in range(2):
            packed = mm(hot, tv[a, :, k * share:(k + 1) * share], ((1,), (0,))).astype(BF)
            sx[a, :, k] = packed.reshape(slots // bucket, bucket, share)
        if a == 0:
            pl.semaphore_wait(barrier, ne + nt - 2)

        @pl.loop(1, ne)
        def _(d):
            to = (me + d) % ne
            rcopy(sx.at[a, to // 2, to % 2], rx.at[a, me], p1s.at[a, to], p1r.at[a, me], (to, t)).start()

        rx[a, me] = sx[a, me // 2, h]

    def own(a, y_, h_):
        return gx.at[a, 4 * y_ + 2 * c + h_]

    own_g = 4 * y + 2 * c + h

    def fan(a, y_, h_, target, part=None):
        g = 4 * y_ + 2 * c + h_
        j = 2 * y_ + h_
        dev = (zdev, ynd, ypd, cdev)[target]
        if part is None:
            ref = gx.at[a, g]
            send(ref, ref, ags.at[a, j, 0, target], agr.at[a, g, 0], dev)
        else:
            ref = gx.at[a, g, pl.ds(part * half, half)]
            send(ref, ref, ags.at[a, j, part, target], agr.at[a, g, part], dev)

    def got(a, y_, h_):
        g = 4 * y_ + 2 * c + h_
        arrived(gx.at[a, g], agr.at[a, g, 0])

    def got_halves(a, y_, h_):
        g = 4 * y_ + 2 * c + h_
        for part in range(2):
            arrived(gx.at[a, g, pl.ds(part * half, half)], agr.at[a, g, part])

    Z, N, B, C = 0, 1, 2, 3
    rows = 128

    def compact(a):
        @pl.loop(1, ne)
        def _(d):
            source = (me + ne - d) % ne
            arrived(rx.at[a, source], p1r.at[a, source])

        buckets = ne * bucket

        @pl.loop(0, cap // rows)
        def _(i):
            at = pl.ds(pl.multiple_of(i * rows, rows), rows)
            pick = (lax.broadcasted_iota(jnp.int32, (rows, buckets), 1) == q_col[at, :]).astype(BF)
            gx[a, own_g, at] = mm(pick, rx[a].reshape(buckets, share), ((1,), (0,))).astype(BF)

    acc[...] = jnp.zeros_like(acc)
    gp[...] = jnp.zeros_like(gp)

    def block_at(g):
        return pl.ds(pl.multiple_of(g * share, share), share)

    def add_x(g):
        x = gx[0, g]
        acc[0] += mm(x, w1v[block_at(g), :], ((1,), (0,)))
        gp[...] += x.astype(F32) * rrow[pl.ds(g, 1), :]

    def add_y(g):
        acc[1] += mm(gx[1, g], w2v[:, block_at(g)], ((1,), (1,)))

    def use(a, y_):
        @pl.loop(0, 2)
        def _(k):
            g = 4 * y_ + 2 * c + k
            o = 4 * y_ + 2 * (1 - c) + k
            (add_x, add_y)[a](g)
            arrived(gx.at[a, o], agr.at[a, o, 0])
            (add_x, add_y)[a](o)

    compact(0)
    fan(0, y, h, Z)
    fan(0, y, h, N)
    fan(0, y, h, B)
    fan(0, y, h, C)
    compact(1)
    fan(1, y, h, N)
    fan(1, y, h, B)
    fan(1, y, h, Z)
    fan(1, y, h, C)
    loads[2].wait()
    loads[3].wait()
    got(0, y, 1 - h)
    fan(0, y, 1 - h, N)
    fan(0, y, 1 - h, B)
    fan(0, y, 1 - h, C)
    got(0, yp, h)
    fan(0, yp, h, N, 0)
    fan(0, yp, h, C)
    got(0, yn, h)
    fan(0, yn, h, B, 1)
    fan(0, yn, h, C)
    got(1, yp, h)
    fan(1, yp, h, N, 0)
    fan(1, yp, h, Z)
    fan(1, yp, h, C)
    got(1, yn, h)
    fan(1, yn, h, B, 1)
    fan(1, yn, h, Z)
    fan(1, yn, h, C)
    use(0, y)
    got(0, yp, 1 - h)
    fan(0, yp, 1 - h, N, 0)
    fan(0, yp, 1 - h, C)
    got(0, yn, 1 - h)
    fan(0, yn, 1 - h, B, 1)
    fan(0, yn, 1 - h, C)
    got_halves(0, yo, h)
    fan(0, yo, h, C)
    got_halves(1, yo, h)
    fan(1, yo, h, Z)
    fan(1, yo, h, C)
    use(0, yp)
    use(0, yn)
    got_halves(0, yo, 1 - h)
    fan(0, yo, 1 - h, C)
    got(1, y, 1 - h)
    fan(1, y, 1 - h, C)
    use(0, yo)
    use(1, y)
    got(1, yp, 1 - h)
    fan(1, yp, 1 - h, C)
    got(1, yn, 1 - h)
    fan(1, yn, 1 - h, C)
    use(1, yp)
    got(1, yo, 1 - h)
    fan(1, yo, 1 - h, C)
    use(1, yn)
    use(1, yo)

    er_rows = 64

    @pl.loop(0, cap // er_rows)
    def _(i):
        at = pl.ds(pl.multiple_of(i * er_rows, er_rows), er_rows)
        gate = jax.nn.sigmoid(jnp.sum(gp[at, :], axis=1, keepdims=True))
        pre = acc[0, at, :]
        up = acc[1, at, :]
        sig = jax.nn.sigmoid(pre)
        hidden = pre * sig
        hg[at, :] = (gate * hidden).astype(BF)
        gate_grad = jnp.sum(hidden * up, axis=1, keepdims=True)
        da[at, :] = (gate * up * sig * (1.0 + pre * (1.0 - sig))).astype(BF)
        score = gate_grad * gate * (1.0 - gate)
        dsb[at, :] = jnp.broadcast_to(score, (er_rows, dsb.shape[1]))

    def r_block(g):
        s = dsb[...]
        wide = jnp.concatenate([s, s], axis=1)
        rb[g] = (mm(da[...], w1v[block_at(g), :], ((1,), (1,))) + wide * rrow[pl.ds(g, 1), :]).astype(BF)

    @pl.loop(0, groups // 2)
    def _(j):
        g = 4 * (j // 2) + 2 * (1 - c) + j % 2
        r_block(g)
        rcopy(rb.at[g], cb.at[j], cs.at[j], cr.at[j], cdev).start()

    s = dsb[...]
    s_hi = s.astype(BF).astype(F32)
    s_mid = (s - s_hi).astype(BF).astype(F32)
    s_lo = s - s_hi - s_mid
    lane = lax.broadcasted_iota(jnp.int32, s.shape, 1)
    terms = jnp.where(lane == 0, s_hi, jnp.where(lane == 1, s_mid, jnp.where(lane == 2, s_lo, 0.0)))
    terms = jnp.transpose(terms)[:16].astype(BF)

    @pl.loop(0, groups)
    def _(g):
        rp[g // 2, g % 2] = mm(terms, gx[0, g], ((1,), (0,)))[:8]

    @pl.loop(1, nt)
    def _(d):
        to = (t + d) % nt
        rcopy(rp.at[to], rq.at[t], r1s.at[to], r1r.at[t], (me, to)).start()

    @pl.loop(0, groups // 2)
    def _(j):
        g = 4 * (j // 2) + 2 * c + j % 2
        r_block(g)

    @pl.loop(0, groups // 2)
    def _(j):
        g = 4 * (j // 2) + 2 * c + j % 2
        arrived(cb.at[j], cr.at[j])
        cb[j] = (cb[j].astype(F32) + rb[g].astype(F32)).astype(BF)

    low = pl.ds(0, half)
    high = pl.ds(half, half)
    for k in range(RING):
        send(cb.at[2 * k + 1 - h, low], zb.at[k], zzs.at[k], zzr.at[k], zdev)
    for k in range(2):
        send(cb.at[2 * yo + k, pl.ds(half, quarter)], yi.at[k, 0], yis.at[k, 0], yir.at[k, 0], ynd)
        send(cb.at[2 * yo + k, pl.ds(half + quarter, quarter)], yi.at[k, 1], yis.at[k, 1], yir.at[k, 1], ypd)

    def weight_grads(first, count):
        @pl.loop(first, first + count)
        def _(g):
            goutv[:, block_at(g)] = mm(hg[...], gx[1, g], ((0,), (0,))).astype(BF)
            ginv[block_at(g), :] = mm(gx[0, g], da[...], ((0,), (0,))).astype(BF)

    @pl.loop(1, nt)
    def _(d):
        source = (t + nt - d) % nt
        arrived(rq.at[source], r1r.at[source])

    rq[t] = rp[t]
    total = rq[0]
    for k in range(1, nt):
        total = total + rq[k]
    rs1[...] = total
    send(rs1.at[1 - h], rz, rzs, rzr, zdev)

    weight_grads(0, 3)
    for k in range(2):
        arrived(yi.at[k, 0], yir.at[k, 0])
        arrived(yi.at[k, 1], yir.at[k, 1])
        first = pl.ds(half, quarter)
        second = pl.ds(half + quarter, quarter)
        cb[2 * yn + k, first] = (cb[2 * yn + k, first].astype(F32) + yi[k, 0].astype(F32)).astype(BF)
        cb[2 * yp + k, second] = (cb[2 * yp + k, second].astype(F32) + yi[k, 1].astype(F32)).astype(BF)
        send(cb.at[2 * yn + k, high], yj.at[k, 0], yjs.at[k, 0], yjr.at[k, 0], ynd)
        send(cb.at[2 * yp + k, high], yj.at[k, 1], yjs.at[k, 1], yjr.at[k, 1], ypd)

    arrived(rz, rzr)
    col = jnp.sum(rs1[h] + rz[...], axis=0, keepdims=True)
    rv[...] = jnp.broadcast_to(col, rv.shape)
    rw[me] = jnp.broadcast_to(col, rv.shape)

    @pl.loop(1, ne)
    def _(d):
        to = (me + d) % ne
        rcopy(rv, rw.at[me], r2s.at[to], r2r.at[me], (to, t)).start()

    weight_grads(3, 4)
    for k in range(RING):
        arrived(zb.at[k], zzr.at[k])

        @pl.when(k != y)
        def _():
            zb[k] = (zb[k].astype(F32) + cb[2 * k + h, low].astype(F32)).astype(BF)

    send(zb.at[yo, pl.ds(0, quarter)], yk.at[0], yks.at[0], ykr.at[0], ynd)
    send(zb.at[yo, pl.ds(quarter, quarter)], yk.at[1], yks.at[1], ykr.at[1], ypd)

    weight_grads(7, 3)
    base = 2 * y + 1 - h
    for k in range(2):
        for side in range(2):
            arrived(yj.at[k, side], yjr.at[k, side])
    cb[base, high] = (
        cb[base, high].astype(F32) + (yj[1 - h, 0].astype(F32) + yj[1 - h, 1].astype(F32))
    ).astype(BF)
    send(cb.at[base, high], zf, zfs, zfr, zdev)
    for side in range(2):
        arrived(yk.at[side], ykr.at[side])
    first = pl.ds(0, quarter)
    second = pl.ds(quarter, quarter)
    zb[yn, first] = (zb[yn, first].astype(F32) + yk[0].astype(F32)).astype(BF)
    zb[yp, second] = (zb[yp, second].astype(F32) + yk[1].astype(F32)).astype(BF)
    send(zb.at[yn], yl.at[0], yls.at[0], ylr.at[0], ynd)
    send(zb.at[yp], yl.at[1], yls.at[1], ylr.at[1], ypd)

    @pl.loop(1, ne)
    def _(d):
        source = (me + ne - d) % ne
        arrived(rw.at[source], r2r.at[source])

    for k in range(ne):
        rxs[k // 2:k // 2 + 1, (k % 2) * share:(k % 2 + 1) * share] = rw[k, 0:1, :]
    ry[t] = rxs[...]

    @pl.loop(1, nt)
    def _(d):
        to = (t + d) % nt
        rcopy(rxs, ry.at[t], r3s.at[to], r3r.at[t], (me, to)).start()

    weight_grads(10, 6)
    out_copies = [
        pltpu.make_async_copy(ginv, gin, outs.at[0]),
        pltpu.make_async_copy(goutv, gout, outs.at[1]),
    ]
    for copy in out_copies:
        copy.start()

    mine = 2 * y + h
    arrived(zf, zfr)
    fb[high, :] = (
        cb[mine, high].astype(F32) + (yj[h, 0].astype(F32) + yj[h, 1].astype(F32)) + zf[...].astype(F32)
    ).astype(BF)
    for side in range(2):
        arrived(yl.at[side], ylr.at[side])
    fb[low, :] = (
        cb[mine, low].astype(F32) + zb[y].astype(F32) + (yl[0].astype(F32) + yl[1].astype(F32))
    ).astype(BF)

    @pl.loop(0, ne * bucket // rows)
    def _(i):
        spread = (
            lax.broadcasted_iota(jnp.int32, (rows, cap), 0) + i * rows == q_row[...]
        ).astype(BF)
        es[pl.ds(i * (rows // bucket), rows // bucket)] = (
            mm(spread, fb[...], ((1,), (0,))).astype(BF).reshape(rows // bucket, bucket, share)
        )

    @pl.loop(1, ne)
    def _(d):
        to = (me + d) % ne
        rcopy(es.at[to], er.at[me // 2, h], rets.at[to], retr.at[me], (to, t)).start()

    er[me // 2, h] = es[me]

    @pl.loop(1, nt)
    def _(d):
        source = (t + nt - d) % nt
        arrived(ry.at[source], r3r.at[source])

    for k in range(nt):
        gr[:, k * feat:(k + 1) * feat] = ry[k]

    @pl.loop(1, ne)
    def _(d):
        source = (me + ne - d) % ne
        arrived(er.at[source // 2, source % 2], retr.at[source])

    home = (lax.broadcasted_iota(jnp.int32, (gt.shape[0], slots), 0) == sel_row[...]).astype(BF)
    for k in range(2):
        gt[:, k * share:(k + 1) * share] = mm(home, er[:, k].reshape(slots, share), ((1,), (0,))).astype(BF)

    @pl.loop(1, ne)
    def _(d):
        to = (me + d) % ne
        for a in range(2):
            rcopy(sx.at[a, 0, 0], rx.at[a, 0], p1s.at[a, to], p1r.at[a, to], zdev).wait_send()
        rcopy(rv, rw.at[0], r2s.at[to], r2r.at[to], zdev).wait_send()
        rcopy(es.at[0], er.at[0, 0], rets.at[to], retr.at[to], zdev).wait_send()

    @pl.loop(1, nt)
    def _(d):
        to = (t + d) % nt
        rcopy(rp.at[0], rq.at[0], r1s.at[to], r1r.at[to], zdev).wait_send()
        rcopy(rxs, ry.at[0], r3s.at[to], r3r.at[to], zdev).wait_send()

    @pl.loop(0, groups // 2)
    def _(j):
        rcopy(rb.at[j], cb.at[j], cs.at[j], cr.at[j], zdev).wait_send()

    for copy in pending:
        copy.wait_send()
    for copy in out_copies:
        copy.wait()


def body(tokens, cotangent, w_in, w_out, router, chosen):
    tok_dev, features = tokens.shape
    hidden = w_in.shape[1]
    ne = lax.axis_size("expert")
    nt = lax.axis_size("tensor")
    bucket = 4 * tok_dev // ne
    experts, cap = chosen.shape
    me = lax.axis_index("expert")
    expert = me // 2
    first = me * tok_dev
    feat = features // nt
    share = feat // 2
    groups = features // share

    starts = jnp.sum((chosen < first).astype(jnp.int32), axis=1)
    place = jnp.arange(cap, dtype=jnp.int32)
    slot = jnp.arange(bucket, dtype=jnp.int32)
    want = starts[:, None] + slot[None, :]
    sel = jnp.sum(
        jnp.where(place[None, None, :] == want[:, :, None], chosen[:, None, :] + 1, 0), axis=2
    ) - 1 - first
    sel = sel.reshape(experts * bucket)
    mine = lax.dynamic_index_in_dim(chosen, expert, 0, keepdims=False)
    home = mine // tok_dev
    before = jnp.sum((mine[None, :] < (home * tok_dev)[:, None]).astype(jnp.int32), axis=1)
    q = home * bucket + place - before
    rrow = lax.dynamic_index_in_dim(router, expert, 1, keepdims=False).astype(F32).reshape(groups, share)

    vm = lambda shape, kind: pltpu.VMEM(shape, kind)
    dma = lambda *shape: pltpu.SemaphoreType.DMA(shape)
    vspec = pl.BlockSpec(memory_space=pltpu.VMEM)
    aspec = pl.BlockSpec(memory_space=pl.ANY)
    half, quarter = cap // 2, cap // 4
    g2 = groups // 2
    scratch = [
        vm((2, tok_dev, feat), BF),
        vm((features, hidden), BF),
        vm((hidden, features), BF),
        vm((2, experts, 2, bucket, share), BF),
        vm((2, ne, bucket, share), BF),
        vm((2, groups, cap, share), BF),
        vm((2, cap, hidden), F32),
        vm((cap, share), F32),
        vm((cap, hidden), BF),
        vm((cap, hidden), BF),
        vm((cap, 128), F32),
        vm((groups, cap, share), BF),
        vm((g2, cap, share), BF),
        vm((RING, half, share), BF),
        vm((2, 2, quarter, share), BF),
        vm((2, 2, half, share), BF),
        vm((2, quarter, share), BF),
        vm((2, half, share), BF),
        vm((half, share), BF),
        vm((8, 128), F32),
        vm((cap, share), BF),
        vm((ne, bucket, share), BF),
        vm((experts, 2, bucket, share), BF),
        vm((features, hidden), BF),
        vm((hidden, features), BF),
        vm((nt, 2, 8, share), F32),
        vm((nt, 2, 8, share), F32),
        vm((2, 8, share), F32),
        vm((8, share), F32),
        vm((8, share), F32),
        vm((ne, 8, share), F32),
        vm((experts, feat), F32),
        vm((nt, experts, feat), F32),
        dma(4), dma(2, ne), dma(2, ne), dma(2, g2, 2, 4), dma(2, groups, 2),
        dma(g2), dma(g2), dma(RING), dma(RING), dma(2, 2), dma(2, 2), dma(2, 2), dma(2, 2),
        dma(2), dma(2), dma(2), dma(2), pltpu.SemaphoreType.DMA, pltpu.SemaphoreType.DMA,
        dma(ne), dma(ne), dma(nt), dma(nt), pltpu.SemaphoreType.DMA, pltpu.SemaphoreType.DMA,
        dma(ne), dma(ne), dma(nt), dma(nt), dma(2),
    ]
    gt, gin, gout, gr = pl.pallas_call(
        functools.partial(step_kernel, ne, nt, bucket),
        out_shape=(
            jax.ShapeDtypeStruct((tok_dev, feat), BF),
            jax.ShapeDtypeStruct((features, hidden), BF),
            jax.ShapeDtypeStruct((hidden, features), BF),
            jax.ShapeDtypeStruct((experts, features), F32),
        ),
        in_specs=[aspec, aspec, aspec, aspec, vspec, vspec, vspec, vspec, vspec],
        out_specs=(vspec, aspec, aspec, vspec),
        scratch_shapes=scratch,
        compiler_params=pltpu.CompilerParams(
            collective_id=0, has_side_effects=True, vmem_limit_bytes=60 * 1024 * 1024
        ),
        name="moe_step",
    )(
        tokens, cotangent, w_in, w_out, rrow,
        sel.reshape(-1, 1), sel.reshape(1, -1), q.reshape(-1, 1), q.reshape(1, -1),
    )
    return gt, gin, gout, gr.T


def solution(mesh):
    placed = (
        P("expert", None),
        P("expert", None),
        P(None, ("expert", "tensor")),
        P(("expert", "tensor"), None),
        P(),
        P(),
    )
    return jax.shard_map(
        body,
        mesh=mesh,
        in_specs=placed,
        out_specs=(
            P("expert", "tensor"),
            P(None, ("expert", "tensor")),
            P(("expert", "tensor"), None),
            P(),
        ),
        check_vma=False,
    )
```

time: 808 us -> 137 us (0.17)
  waiting for transfers between devices: 444 us -> 0 us
  blocking collectives: 193 us -> 0 us
  Pallas kernels: 0 us -> 121 us
  local copies, waits for them, and re-layouts: 65.6 us -> 10.9 us
  other arithmetic: 43 us -> 4.86 us
  matrix products: 25.8 us -> 0 us
  starting transfers between devices: 18.8 us -> 0 us
  between operations: 15.7 us -> 0.7 us
    psum x1 -> x0, waiting for transfers between devices: 204 us -> none  [body(): grad_router = lax.psum(router_term, ('expert', 'tensor'))]
    all_to_all x1 -> x0, blocking collectives: 193 us -> none  [body(): lax.all_to_all(pack(tokens), 'expert', split_axis=0, concat_axis=0, tiled...]
    all_to_all x2 -> x0, waiting for transfers between devices: 179 us -> none  [the longest x1 142 us: body(): lax.all_to_all(pack(cotangent), 'expert', split_axis=0, concat_axis=0, ti...]
    pallas_call x0 -> x1, Pallas kernels: none -> 121 us  [body(): pl.pallas_call(functools.partial(step_kernel, ne, nt, bucket), out_shape=...]
    reduce_scatter x1 -> x0, waiting for transfers between devices: 60.2 us -> none  [body(): lax.psum_scatter(jnp.dot(w_in, pre_grad.T, preferred_element_type=jnp.flo...]
    gather x11 -> x0, local copies, waits for them, and re-layouts: 58.4 us -> none  [the longest x2 24.8 us: pack(): source[send_rows]]
    dot_general x7 -> x0, matrix products: 25.8 us -> none  [the longest x1 5.12 us: body(): jnp.dot(w_in, pre_grad.T, preferred_element_type=jnp.float32)]
    gather x7 -> x0, other arithmetic: 20.1 us -> none  [the longest x3 20 us: body(): run_start[home_index]]
  transfers between devices with their start and end apart: 4 -> 0, of which waited for: 4 -> 0; matrix products, arithmetic and copies ran while one was open for 8% -> 0% of each run, Pallas kernels for 0% -> 0%
where the time goes in v1:
time: 137 us
  Pallas kernels  121 us (88%)
  local copies, waits for them, and re-layouts  10.9 us (8%)
  other arithmetic  4.86 us (4%)
    pallas_call x1, Pallas kernels, body(): pl.pallas_call(functools.partial(step_kernel, ne, nt, bucket), out_shape=...  121 us
    unnamed x8, local copies, waits for them, and re-layouts  6.89 us

profile of v1, /device:TPU:1, one launch (start us, length us, event | category | flops | bytes accessed | tf_op | source)
XLA Modules:
  0.0 137.1 jit_solution(11475101026462046534)
XLA Ops:
  0.6 0.7 fusion.8
  1.4 0.7 constant_dynamic-slice_fusion
  2.1 0.2 convert_reduce_fusion
  2.4 1.3 add_subtract_fusion.1.q_row
  3.7 0.9 convert_reduce_fusion.2
  4.6 0.6 reshape.170.rrow
  5.2 0.9 convert_reduce_fusion.1
  6.0 0.1 iota_add_fusion
  6.1 0.6 select_reduce_fusion
  6.7 0.7 sub.62.sel_row
  7.4 1.0 sub.68.sel_col
  8.3 0.1 copy.22
  8.5 0.1 copy.27
  8.6 0.9 fusion.3.q_col
  9.5 120.6 %moe_step.1 = (bf16[256,512]{1,0:T(8,128)(2,1)}, bf16[4096,256]{1,0:T(8,128)(2,1)}, bf16[256,4096]{1,0:T(8,128)(2,1)}, f32[16,4096]{1,0:T(8,128)}) custom-call(bf16[256,4096]{1,0:T(8,128)(2,1)} %tok.1, bf16[256,4096]{1,0:T(8,128)(2,1)} %cot.1, bf16[4096,256]{1,0:T(8,128)(2,1)} %w_in.1, bf16[256,4096]{1,0:T(8,128)(2,1)} %w_out.1, f32[16,256]{1,0:T(8,128)} %reshape.170.rrow, ...), custom_call_target="tpu_custom_call" | custom-call | tf_op jit(solution)/shard_map/moe_step/pallas_call | solution.py:521
  130.2 1.7 %copy.33 = bf16[256,512]{1,0:T(8,128)(2,1)} copy(bf16[256,512]{1,0:T(8,128)(2,1)} %get-tuple-element.18) | data formatting | bytes 524288
  131.8 0.0 copy-start
  131.8 3.2 %copy.34 = bf16[4096,256]{1,0:T(8,128)(2,1)} copy(bf16[4096,256]{1,0:T(8,128)(2,1)} %get-tuple-element.19) | data formatting | bytes 4194304
  135.0 0.0 copy-done
  135.0 0.0 copy-start.1
  135.0 1.3 copy.35
  136.4 0.0 copy-done.1
  136.4 0.7 copy.36
  (2 shorter events, 0.0 us)
Async XLA Ops:
  131.8 3.2 %copy-start = (bf16[256,4096]{1,0:T(8,128)(2,1)S(1)}, bf16[256,4096]{1,0:T(8,128)(2,1)}, u32[]{:S(2)}) copy-start(bf16[256,4096]{1,0:T(8,128)(2,1)} %get-tuple-element.20) | copy-start | bytes 6291460
  135.0 1.3 copy-start.1

commit v2 on v1

--- a/solution.py
+++ b/solution.py
@@ -19,11 +19,12 @@
 
 def step_kernel(
     ne, nt, bucket,
-    tok, cot, w_in, w_out, rrow, sel_col, sel_row, q_col, q_row,
+    tok, cot, w_in, w_out, rt, chosen,
     gt, gin, gout, gr,
+    chf, rrow, hot, q_row, q_col,
     tv, w1v, w2v, sx, rx, gx, acc, gp, hg, da, dsb, rb, cb, zb, yi, yj, yk, yl, zf, fv, fb, es, er,
     ginv, goutv, rp, rq, rs1, rz, rv, rw, rxs, ry,
-    ld, p1s, p1r, ags, agr, cs, cr, zzs, zzr, yis, yir, yjs, yjr, yks, ykr, yls, ylr, zfs, zfr,
+    ld, p1s, p1r, fws, pcs, pcr, ags, agr, cs, cr, zzs, zzr, yis, yir, yjs, yjr, yks, ykr, yls, ylr, zfs, zfr,
     rets, retr, r1s, r1r, rzs, rzr, r2s, r2r, r3s, r3r, outs,
 ):
     me = lax.axis_index("expert")
@@ -80,26 +81,64 @@
     def _(d):
         pl.semaphore_signal(barrier, inc=1, device_id=(me, (t + d) % nt), device_id_type=MESH)
 
-    slots = sel_col.shape[0]
-    hot = (lax.broadcasted_iota(jnp.int32, (slots, tv.shape[1]), 1) == sel_col[...]).astype(BF)
+    experts = chosen.shape[0]
+    tok_dev = tv.shape[1]
+    slots = experts * bucket
+    zr = ne // RING
+    x = me // zr
+    z = me % zr
+    first = (me * tok_dev).astype(F32)
+    chf[...] = chosen[...].astype(F32)
+    col = lax.broadcasted_iota(jnp.int32, (bucket, cap), 1).astype(F32)
+    row = lax.broadcasted_iota(jnp.int32, (bucket, cap), 0).astype(F32)
+    tok_at = lax.broadcasted_iota(jnp.int32, (bucket, tok_dev), 1).astype(F32)
+
+    @pl.loop(0, experts)
+    def _(k):
+        picks = chf[pl.ds(k, 1), :]
+        start = jnp.sum(jnp.where(picks < first, 1.0, 0.0), axis=1, keepdims=True)
+        held = jnp.sum(jnp.where(col == row + start, picks + 1.0, 0.0), axis=1, keepdims=True) - 1.0 - first
+        hot[pl.ds(pl.multiple_of(k * bucket, bucket), bucket), :] = jnp.where(tok_at == held, 1.0, 0.0).astype(BF)
 
     for a in range(2):
         loads[a].wait()
         for k in range(2):
-            packed = mm(hot, tv[a, :, k * share:(k + 1) * share], ((1,), (0,))).astype(BF)
+            packed = mm(hot[...], tv[a, :, k * share:(k + 1) * share], ((1,), (0,))).astype(BF)
             sx[a, :, k] = packed.reshape(slots // bucket, bucket, share)
         if a == 0:
             pl.semaphore_wait(barrier, ne + nt - 2)
 
-        @pl.loop(1, ne)
-        def _(d):
-            to = (me + d) % ne
-            rcopy(sx.at[a, to // 2, to % 2], rx.at[a, me], p1s.at[a, to], p1r.at[a, me], (to, t)).start()
-
-        rx[a, me] = sx[a, me // 2, h]
-
-    def own(a, y_, h_):
-        return gx.at[a, 4 * y_ + 2 * c + h_]
+        @pl.loop(0, experts)
+        def _(k):
+            target = (x * (zr // 2) + z // 2 + k) % experts
+            near = ((2 * target) % zr + zr - z) % zr // (zr // 2)
+            to = 2 * target + near
+
+            @pl.when(to != me)
+            def _():
+                rcopy(sx.at[a, target], rx.at[a, me], p1s.at[a, target], p1r.at[a, me], (to, t)).start()
+
+            @pl.when(to == me)
+            def _():
+                rx[a, me] = sx[a, target]
+
+    home_row = lax.broadcasted_iota(jnp.int32, (ne, cap), 0).astype(F32)
+    place = lax.broadcasted_iota(jnp.int32, (ne, cap), 1).astype(F32)
+    mine_row = chf[pl.ds(me // 2, 1), :]
+    low_bound = home_row * float(tok_dev)
+    before = jnp.sum(jnp.where(mine_row < low_bound, 1.0, 0.0), axis=1, keepdims=True)
+    inside = jnp.logical_and(mine_row >= low_bound, mine_row < low_bound + float(tok_dev))
+    q = jnp.sum(jnp.where(inside, home_row * float(bucket) + place - before, 0.0), axis=0, keepdims=True)
+    q_row[...] = jnp.broadcast_to(q, q_row.shape)
+    q_col[...] = jnp.transpose(jnp.broadcast_to(q, (128, cap)))
+    router_all = rt[...].astype(F32)
+    rrow[...] = jnp.broadcast_to(
+        jnp.sum(
+            jnp.where(lax.broadcasted_iota(jnp.int32, router_all.shape, 0) == me // 2, router_all, 0.0),
+            axis=0, keepdims=True,
+        ),
+        rrow.shape,
+    )
 
     own_g = 4 * y + 2 * c + h
 
@@ -126,19 +165,38 @@
     Z, N, B, C = 0, 1, 2, 3
     rows = 128
 
+    buckets = ne * bucket
+    zdir = 1 - 2 * h
+
+    def near_home(i, toward):
+        zz = (z + zr + toward * (i // RING) + (toward + zdir) // 2) % zr
+        return ((x + i) % RING) * zr + zz
+
+    def near_rows(a, first_i, count):
+        @pl.loop(first_i, first_i + count)
+        def _(i):
+            source = near_home(i, -zdir)
+
+            @pl.when(source != me)
+            def _():
+                arrived(rx.at[a, source], p1r.at[a, source])
+
+            ref = rx.at[a, source, 1 - h]
+            rcopy(ref, ref, fws.at[a, source], p1r.at[a, source], zdev).start()
+
+    def far_rows(a):
+        @pl.loop(0, ne // 2)
+        def _(i):
+            source = near_home(i, zdir)
+            arrived(rx.at[a, source, h], p1r.at[a, source])
+
     def compact(a):
-        @pl.loop(1, ne)
-        def _(d):
-            source = (me + ne - d) % ne
-            arrived(rx.at[a, source], p1r.at[a, source])
-
-        buckets = ne * bucket
-
         @pl.loop(0, cap // rows)
         def _(i):
             at = pl.ds(pl.multiple_of(i * rows, rows), rows)
-            pick = (lax.broadcasted_iota(jnp.int32, (rows, buckets), 1) == q_col[at, :]).astype(BF)
-            gx[a, own_g, at] = mm(pick, rx[a].reshape(buckets, share), ((1,), (0,))).astype(BF)
+            slot = lax.broadcasted_iota(jnp.int32, (rows, buckets), 1).astype(F32)
+            pick = jnp.where(slot == q_col[at, 0:1], 1.0, 0.0).astype(BF)
+            gx[a, own_g, at] = mm(pick, rx[a, :, h].reshape(buckets, share), ((1,), (0,))).astype(BF)
 
     acc[...] = jnp.zeros_like(acc)
     gp[...] = jnp.zeros_like(gp)
@@ -149,7 +207,7 @@
     def add_x(g):
         x = gx[0, g]
         acc[0] += mm(x, w1v[block_at(g), :], ((1,), (0,)))
-        gp[...] += x.astype(F32) * rrow[pl.ds(g, 1), :]
+        gp[...] += x.astype(F32) * rrow[0:1, block_at(g)]
 
     def add_y(g):
         acc[1] += mm(gx[1, g], w2v[:, block_at(g)], ((1,), (1,)))
@@ -163,18 +221,18 @@
             arrived(gx.at[a, o], agr.at[a, o, 0])
             (add_x, add_y)[a](o)
 
+    def got_half(a, y_, h_, part):
+        g = 4 * y_ + 2 * c + h_
+        arrived(gx.at[a, g, pl.ds(part * half, half)], agr.at[a, g, part])
+
+    near_rows(0, 0, ne // 2)
+    far_rows(0)
     compact(0)
-    fan(0, y, h, Z)
     fan(0, y, h, N)
     fan(0, y, h, B)
+    fan(0, y, h, Z)
     fan(0, y, h, C)
-    compact(1)
-    fan(1, y, h, N)
-    fan(1, y, h, B)
-    fan(1, y, h, Z)
-    fan(1, y, h, C)
-    loads[2].wait()
-    loads[3].wait()
+    near_rows(1, 0, ne // 4)
     got(0, y, 1 - h)
     fan(0, y, 1 - h, N)
     fan(0, y, 1 - h, B)
@@ -185,15 +243,18 @@
     got(0, yn, h)
     fan(0, yn, h, B, 1)
     fan(0, yn, h, C)
-    got(1, yp, h)
-    fan(1, yp, h, N, 0)
-    fan(1, yp, h, Z)
-    fan(1, yp, h, C)
-    got(1, yn, h)
-    fan(1, yn, h, B, 1)
-    fan(1, yn, h, Z)
-    fan(1, yn, h, C)
+    near_rows(1, ne // 4, ne // 4)
+    loads[2].wait()
     use(0, y)
+    far_rows(1)
+    compact(1)
+    fan(1, y, h, Z, 1)
+    fan(1, y, h, N, 0)
+    fan(1, y, h, B, 0)
+    fan(1, y, h, N, 1)
+    fan(1, y, h, B, 1)
+    fan(1, y, h, Z, 0)
+    fan(1, y, h, C)
     got(0, yp, 1 - h)
     fan(0, yp, 1 - h, N, 0)
     fan(0, yp, 1 - h, C)
@@ -202,23 +263,60 @@
     fan(0, yn, 1 - h, C)
     got_halves(0, yo, h)
     fan(0, yo, h, C)
-    got_halves(1, yo, h)
-    fan(1, yo, h, Z)
-    fan(1, yo, h, C)
     use(0, yp)
-    use(0, yn)
+    got_half(1, y, 1 - h, 1)
+    fan(1, y, 1 - h, N, 1)
+    fan(1, y, 1 - h, B, 1)
+    loads[3].wait()
+    eighth = half // 2
+
+    def piece(a, y_, h_, part, k):
+        g = 4 * y_ + 2 * c + h_
+        return gx.at[a, g, pl.ds(part * half + k * eighth, eighth)]
+
+    def relay(y_, h_, part, k, target):
+        g = 4 * y_ + 2 * c + h_
+        ref = piece(1, y_, h_, part, k)
+        send(ref, ref, pcs.at[h_, part, k], pcr.at[h_, part, k], (zdev, ynd, ypd, cdev)[target])
+
+    def got_pieces(y_, h_, part):
+        for k in range(2):
+            arrived(piece(1, y_, h_, part, k), pcr.at[h_, part, k])
+
+    got_half(1, yp, h, 0)
+    relay(yp, h, 0, 0, N)
+    fan(1, yp, h, Z, 0)
+    got_half(1, yn, h, 0)
+    relay(yn, h, 0, 1, B)
+    fan(1, yn, h, Z, 0)
     got_halves(0, yo, 1 - h)
     fan(0, yo, 1 - h, C)
-    got(1, y, 1 - h)
+    use(0, yn)
+    got_half(1, yp, h, 1)
+    relay(yp, h, 1, 0, N)
+    fan(1, yp, h, C)
+    got_half(1, yn, h, 1)
+    relay(yn, h, 1, 1, B)
+    fan(1, yn, h, C)
+    got_half(1, y, 1 - h, 0)
     fan(1, y, 1 - h, C)
     use(0, yo)
+    got_pieces(yo, h, 0)
+    fan(1, yo, h, Z, 0)
+    got_half(1, yp, 1 - h, 1)
+    relay(yp, 1 - h, 1, 0, N)
+    got_half(1, yn, 1 - h, 1)
+    relay(yn, 1 - h, 1, 1, B)
     use(1, y)
-    got(1, yp, 1 - h)
+    got_half(1, yp, 1 - h, 0)
     fan(1, yp, 1 - h, C)
-    got(1, yn, 1 - h)
+    got_half(1, yn, 1 - h, 0)
     fan(1, yn, 1 - h, C)
+    got_pieces(yo, h, 1)
+    fan(1, yo, h, C)
     use(1, yp)
-    got(1, yo, 1 - h)
+    got_half(1, yo, 1 - h, 0)
+    got_pieces(yo, 1 - h, 1)
     fan(1, yo, 1 - h, C)
     use(1, yn)
     use(1, yo)
@@ -239,16 +337,17 @@
         score = gate_grad * gate * (1.0 - gate)
         dsb[at, :] = jnp.broadcast_to(score, (er_rows, dsb.shape[1]))
 
-    def r_block(g):
+    def r_value(g):
         s = dsb[...]
         wide = jnp.concatenate([s, s], axis=1)
-        rb[g] = (mm(da[...], w1v[block_at(g), :], ((1,), (1,))) + wide * rrow[pl.ds(g, 1), :]).astype(BF)
+        return mm(da[...], w1v[block_at(g), :], ((1,), (1,))) + wide * rrow[0:1, block_at(g)]
 
     @pl.loop(0, groups // 2)
     def _(j):
-        g = 4 * (j // 2) + 2 * (1 - c) + j % 2
-        r_block(g)
-        rcopy(rb.at[g], cb.at[j], cs.at[j], cr.at[j], cdev).start()
+        place_y = (yo + j // 2) % RING
+        i = 2 * place_y + j % 2
+        rb[i] = r_value(4 * place_y + 2 * (1 - c) + j % 2).astype(BF)
+        rcopy(rb.at[i], cb.at[i], cs.at[i], cr.at[i], cdev).start()
 
     s = dsb[...]
     s_hi = s.astype(BF).astype(F32)
@@ -267,24 +366,21 @@
         to = (t + d) % nt
         rcopy(rp.at[to], rq.at[t], r1s.at[to], r1r.at[t], (me, to)).start()
 
-    @pl.loop(0, groups // 2)
-    def _(j):
-        g = 4 * (j // 2) + 2 * c + j % 2
-        r_block(g)
-
-    @pl.loop(0, groups // 2)
-    def _(j):
-        g = 4 * (j // 2) + 2 * c + j % 2
-        arrived(cb.at[j], cr.at[j])
-        cb[j] = (cb[j].astype(F32) + rb[g].astype(F32)).astype(BF)
-
     low = pl.ds(0, half)
     high = pl.ds(half, half)
-    for k in range(RING):
-        send(cb.at[2 * k + 1 - h, low], zb.at[k], zzs.at[k], zzr.at[k], zdev)
-    for k in range(2):
-        send(cb.at[2 * yo + k, pl.ds(half, quarter)], yi.at[k, 0], yis.at[k, 0], yir.at[k, 0], ynd)
-        send(cb.at[2 * yo + k, pl.ds(half + quarter, quarter)], yi.at[k, 1], yis.at[k, 1], yir.at[k, 1], ypd)
+    for place_y in (yo, yp, y, yn):
+        @pl.loop(0, 2)
+        def _(k):
+            j = 2 * place_y + k
+            value = r_value(4 * place_y + 2 * c + k)
+            arrived(cb.at[j], cr.at[j])
+            cb[j] = (cb[j].astype(F32) + value).astype(BF)
+
+        if place_y is yo:
+            for k in range(2):
+                send(cb.at[2 * yo + k, pl.ds(half, quarter)], yi.at[k, 0], yis.at[k, 0], yir.at[k, 0], ynd)
+                send(cb.at[2 * yo + k, pl.ds(half + quarter, quarter)], yi.at[k, 1], yis.at[k, 1], yir.at[k, 1], ypd)
+        send(cb.at[2 * place_y + 1 - h, low], zb.at[place_y], zzs.at[place_y], zzr.at[place_y], zdev)
 
     def weight_grads(first, count):
         @pl.loop(first, first + count)
@@ -390,7 +486,7 @@
     @pl.loop(0, ne * bucket // rows)
     def _(i):
         spread = (
-            lax.broadcasted_iota(jnp.int32, (rows, cap), 0) + i * rows == q_row[...]
+            (lax.broadcasted_iota(jnp.int32, (rows, cap), 0) + i * rows).astype(F32) == q_row[0:1, :]
         ).astype(BF)
         es[pl.ds(i * (rows // bucket), rows // bucket)] = (
             mm(spread, fb[...], ((1,), (0,))).astype(BF).reshape(rows // bucket, bucket, share)
@@ -416,17 +512,30 @@
         source = (me + ne - d) % ne
         arrived(er.at[source // 2, source % 2], retr.at[source])
 
-    home = (lax.broadcasted_iota(jnp.int32, (gt.shape[0], slots), 0) == sel_row[...]).astype(BF)
     for k in range(2):
-        gt[:, k * share:(k + 1) * share] = mm(home, er[:, k].reshape(slots, share), ((1,), (0,))).astype(BF)
+        gt[:, k * share:(k + 1) * share] = mm(hot[...], er[:, k].reshape(slots, share), ((0,), (0,))).astype(BF)
 
     @pl.loop(1, ne)
     def _(d):
         to = (me + d) % ne
-        for a in range(2):
-            rcopy(sx.at[a, 0, 0], rx.at[a, 0], p1s.at[a, to], p1r.at[a, to], zdev).wait_send()
         rcopy(rv, rw.at[0], r2s.at[to], r2r.at[to], zdev).wait_send()
         rcopy(es.at[0], er.at[0, 0], rets.at[to], retr.at[to], zdev).wait_send()
+
+    @pl.loop(0, experts)
+    def _(k):
+        near = ((2 * k) % zr + zr - z) % zr // (zr // 2)
+
+        @pl.when(2 * k + near != me)
+        def _():
+            for a in range(2):
+                rcopy(sx.at[a, 0], rx.at[a, 0], p1s.at[a, k], p1r.at[a, 0], zdev).wait_send()
+
+    @pl.loop(0, ne // 2)
+    def _(i):
+        source = near_home(i, -zdir)
+        for a in range(2):
+            ref = rx.at[a, source, 1 - h]
+            rcopy(ref, ref, fws.at[a, source], p1r.at[a, source], zdev).wait_send()
 
     @pl.loop(1, nt)
     def _(d):
@@ -442,6 +551,39 @@
         copy.wait_send()
     for copy in out_copies:
         copy.wait()
+
+
+def hand_kernel(*refs):
+    ins, outs, bufs = refs[:4], refs[4:8], refs[8:12]
+    sin, sout = refs[12], refs[13]
+    copies = []
+    for n, (src, buf, dst) in enumerate(zip(ins, bufs, outs)):
+        parts = 4 if src.shape[0] * src.shape[1] >= 1 << 19 else 1
+        step = src.shape[0] // parts
+        for k in range(parts):
+            at = pl.ds(k * step, step)
+            there = pltpu.make_async_copy(src.at[at], buf.at[at], sin.at[n, k])
+            back = pltpu.make_async_copy(buf.at[at], dst.at[at], sout.at[n, k])
+            there.start()
+            copies.append((there, back))
+    for there, back in copies:
+        there.wait()
+        back.start()
+    for _, back in copies:
+        back.wait()
+
+
+def hand_out(*arrays):
+    aspec = pl.BlockSpec(memory_space=pl.ANY)
+    return pl.pallas_call(
+        hand_kernel,
+        out_shape=tuple(jax.ShapeDtypeStruct(v.shape, v.dtype) for v in arrays),
+        in_specs=[aspec] * 4,
+        out_specs=(aspec,) * 4,
+        scratch_shapes=[pltpu.VMEM(v.shape, v.dtype) for v in arrays]
+        + [pltpu.SemaphoreType.DMA((4, 4)), pltpu.SemaphoreType.DMA((4, 4))],
+        name="hand_out",
+    )(*arrays)
 
 
 def body(tokens, cotangent, w_in, w_out, router, chosen):
@@ -451,26 +593,9 @@
     nt = lax.axis_size("tensor")
     bucket = 4 * tok_dev // ne
     experts, cap = chosen.shape
-    me = lax.axis_index("expert")
-    expert = me // 2
-    first = me * tok_dev
     feat = features // nt
     share = feat // 2
     groups = features // share
-
-    starts = jnp.sum((chosen < first).astype(jnp.int32), axis=1)
-    place = jnp.arange(cap, dtype=jnp.int32)
-    slot = jnp.arange(bucket, dtype=jnp.int32)
-    want = starts[:, None] + slot[None, :]
-    sel = jnp.sum(
-        jnp.where(place[None, None, :] == want[:, :, None], chosen[:, None, :] + 1, 0), axis=2
-    ) - 1 - first
-    sel = sel.reshape(experts * bucket)
-    mine = lax.dynamic_index_in_dim(chosen, expert, 0, keepdims=False)
-    home = mine // tok_dev
-    before = jnp.sum((mine[None, :] < (home * tok_dev)[:, None]).astype(jnp.int32), axis=1)
-    q = home * bucket + place - before
-    rrow = lax.dynamic_index_in_dim(router, expert, 1, keepdims=False).astype(F32).reshape(groups, share)
 
     vm = lambda shape, kind: pltpu.VMEM(shape, kind)
     dma = lambda *shape: pltpu.SemaphoreType.DMA(shape)
@@ -479,18 +604,23 @@
     half, quarter = cap // 2, cap // 4
     g2 = groups // 2
     scratch = [
+        vm((experts, cap), F32),
+        vm((8, features), F32),
+        vm((experts * bucket, tok_dev), BF),
+        vm((8, cap), F32),
+        vm((cap, 128), F32),
         vm((2, tok_dev, feat), BF),
         vm((features, hidden), BF),
         vm((hidden, features), BF),
         vm((2, experts, 2, bucket, share), BF),
-        vm((2, ne, bucket, share), BF),
+        vm((2, ne, 2, bucket, share), BF),
         vm((2, groups, cap, share), BF),
         vm((2, cap, hidden), F32),
         vm((cap, share), F32),
         vm((cap, hidden), BF),
         vm((cap, hidden), BF),
         vm((cap, 128), F32),
-        vm((groups, cap, share), BF),
+        vm((g2, cap, share), BF),
         vm((g2, cap, share), BF),
         vm((RING, half, share), BF),
         vm((2, 2, quarter, share), BF),
@@ -512,7 +642,7 @@
         vm((ne, 8, share), F32),
         vm((experts, feat), F32),
         vm((nt, experts, feat), F32),
-        dma(4), dma(2, ne), dma(2, ne), dma(2, g2, 2, 4), dma(2, groups, 2),
+        dma(4), dma(2, experts), dma(2, ne), dma(2, ne), dma(2, 2, 2), dma(2, 2, 2), dma(2, g2, 2, 4), dma(2, groups, 2),
         dma(g2), dma(g2), dma(RING), dma(RING), dma(2, 2), dma(2, 2), dma(2, 2), dma(2, 2),
         dma(2), dma(2), dma(2), dma(2), pltpu.SemaphoreType.DMA, pltpu.SemaphoreType.DMA,
         dma(ne), dma(ne), dma(nt), dma(nt), pltpu.SemaphoreType.DMA, pltpu.SemaphoreType.DMA,
@@ -526,7 +656,7 @@
             jax.ShapeDtypeStruct((hidden, features), BF),
             jax.ShapeDtypeStruct((experts, features), F32),
         ),
-        in_specs=[aspec, aspec, aspec, aspec, vspec, vspec, vspec, vspec, vspec],
+        in_specs=[aspec, aspec, aspec, aspec, vspec, vspec],
         out_specs=(vspec, aspec, aspec, vspec),
         scratch_shapes=scratch,
         compiler_params=pltpu.CompilerParams(
@@ -534,9 +664,9 @@
         ),
         name="moe_step",
     )(
-        tokens, cotangent, w_in, w_out, rrow,
-        sel.reshape(-1, 1), sel.reshape(1, -1), q.reshape(-1, 1), q.reshape(1, -1),
+        tokens, cotangent, w_in, w_out, router.T, chosen,
     )
+    gt, gin, gout, gr = hand_out(gt, gin, gout, gr)
     return gt, gin, gout, gr.T
 
 

time: 137 us -> 131 us (0.956)
  local copies, waits for them, and re-layouts: 10.9 us -> 0 us
  Pallas kernels: 121 us -> 130 us
  other arithmetic: 4.86 us -> 0 us
    unnamed x8 -> x0, local copies, waits for them, and re-layouts: 6.89 us -> none
    pallas_call x1, Pallas kernels: 121 us -> 126 us  [body(): pl.pallas_call(functools.partial(step_kernel, ne, nt, bucket), out_shape=...]
    pallas_call x0 -> x1, Pallas kernels: none -> 4.3 us  [hand_out(): pl.pallas_call(hand_kernel, out_shape=tuple((jax.ShapeDtypeStruct(v.shape...]
    sub x3 -> x0, other arithmetic: 2.2 us -> none  [the longest x2 2.19 us: body(): q = home * bucket + place - before]
    reduce_sum x3 -> x0, other arithmetic: 1.68 us -> none  [the longest x1 0.87 us: body(): starts = jnp.sum((chosen < first).astype(jnp.int32), axis=1)]
    sub x2 -> x0, local copies, waits for them, and re-layouts: 1.62 us -> none  [body(): jnp.sum(jnp.where(place[None, None, :] == want[:, :, None], chosen[:, Non...]
where the time goes in v2:
time: 131 us; the launch traced here: 130 us
  Pallas kernels  130 us (99%)
    pallas_call x1, Pallas kernels, body(): pl.pallas_call(functools.partial(step_kernel, ne, nt, bucket), out_shape=...  126 us
    pallas_call x1, Pallas kernels, hand_out(): pl.pallas_call(hand_kernel, out_shape=tuple((jax.ShapeDtypeStruct(v.shape...  4.3 us

profile of v2, /device:TPU:1, one launch (start us, length us, event | category | flops | bytes accessed | tf_op | source)
XLA Modules:
  0.0 130.4 jit_solution(2902369486409268410)
XLA Ops:
  0.6 125.5 %moe_step.1 = (bf16[256,512]{1,0:T(8,128)(2,1)}, bf16[4096,256]{1,0:T(8,128)(2,1)}, bf16[256,4096]{1,0:T(8,128)(2,1)}, f32[16,4096]{1,0:T(8,128)}) custom-call(bf16[256,4096]{1,0:T(8,128)(2,1)} %tok.1, bf16[256,4096]{1,0:T(8,128)(2,1)} %cot.1, bf16[4096,256]{1,0:T(8,128)(2,1)} %w_in.1, bf16[256,4096]{1,0:T(8,128)(2,1)} %w_out.1, bf16[16,4096]{1,0:T(8,128)(2,1)} %bitcast.2, ...), custom_call_target="tpu_custom_call" | custom-call | tf_op jit(solution)/shard_map/moe_step/pallas_call | solution.py:651
  126.2 4.3 %hand_out.1 = (bf16[256,512]{1,0:T(8,128)(2,1)}, bf16[4096,256]{1,0:T(8,128)(2,1)}, bf16[256,4096]{1,0:T(8,128)(2,1)}, f32[16,4096]{1,0:T(8,128)}) custom-call(bf16[256,512]{1,0:T(8,128)(2,1)} %get-tuple-element.12.refs_0_, bf16[4096,256]{1,0:T(8,128)(2,1)} %get-tuple-element.13.refs_1_, bf16[256,4096]{1,0:T(8,128)(2,1)} %get-tuple-element.14.refs_2_, ...), custom_call_target="tpu_custom_call" | custom-call | tf_op jit(solution)/shard_map/hand_out/pallas_call | solution.py:578

commit v3 on v1

v3 whole, which is shorter than its diff:
```python
import functools

import jax
import jax.numpy as jnp
from jax import lax
from jax.experimental import pallas as pl
from jax.experimental.pallas import tpu as pltpu
from jax.sharding import PartitionSpec as P

MESH = pl.DeviceIdType.MESH
BF = jnp.bfloat16
F32 = jnp.float32
RING = 4


def mm(a, b, dims):
    return lax.dot_general(a, b, (dims, ((), ())), preferred_element_type=F32)


def step_kernel(
    ne, nt, bucket,
    tok, cot, w_in, w_out, rt_any, chosen_any,
    gt, gin, gout, gr,
    chosen, rt, rrow, hot, q_row, q_col,
    tv, w1v, w2v, sx, rx, gx, acc, gp, hg, da, dsb, rb, cb, zb, yi, yj, yk, yl, zf, fv, fb, es, er,
    ginv, goutv, rp, rq, rs1, rz, rv, rw, rxs, ry,
    ld, p1s, p1r, pcs, pcr, ags, agr, cs, cr, zzs, zzr, yis, yir, yjs, yjr, yks, ykr, yls, ylr, zfs, zfr,
    rets, retr, r1s, r1r, rzs, rzr, r2s, r2r, r3s, r3r, outs,
):
    me = lax.axis_index("expert")
    t = lax.axis_index("tensor")
    h = me % 2
    y = t // 2
    c = t % 2
    feat = tv.shape[2]
    share = feat // 2
    cap = hg.shape[0]
    groups = gx.shape[1]
    half = cap // 2
    quarter = cap // 4

    zdev = (me + 1 - 2 * h, t)
    cdev = (me, 2 * y + 1 - c)
    yn = (y + 1) % RING
    yp = (y + 3) % RING
    yo = (y + 2) % RING
    ynd = (me, 2 * yn + c)
    ypd = (me, 2 * yp + c)

    def rcopy(src, dst, ss, rs, dev):
        return pltpu.make_async_remote_copy(
            src_ref=src, dst_ref=dst, send_sem=ss, recv_sem=rs, device_id=dev, device_id_type=MESH
        )

    pending = []

    def send(src, dst, ss, rs, dev):
        copy = rcopy(src, dst, ss, rs, dev)
        copy.start()
        pending.append(copy)

    def arrived(dst, rs):
        rcopy(dst, dst, rs, rs, zdev).wait_recv()

    loads = [
        pltpu.make_async_copy(tok.at[:, pl.ds(pl.multiple_of(t * feat, feat), feat)], tv.at[0], ld.at[0]),
        pltpu.make_async_copy(cot.at[:, pl.ds(pl.multiple_of(t * feat, feat), feat)], tv.at[1], ld.at[1]),
        pltpu.make_async_copy(w_in, w1v, ld.at[2]),
        pltpu.make_async_copy(w_out, w2v, ld.at[3]),
    ]
    load_chosen = pltpu.make_async_copy(chosen_any, chosen, ld.at[4])
    load_router = pltpu.make_async_copy(rt_any, rt, ld.at[5])
    load_chosen.start()
    loads[0].start()
    loads[1].start()
    load_router.start()
    loads[2].start()
    loads[3].start()

    barrier = pltpu.get_barrier_semaphore()

    @pl.loop(1, ne)
    def _(d):
        pl.semaphore_signal(barrier, inc=1, device_id=((me + d) % ne, t), device_id_type=MESH)

    @pl.loop(1, nt)
    def _(d):
        pl.semaphore_signal(barrier, inc=1, device_id=(me, (t + d) % nt), device_id_type=MESH)

    experts = chosen.shape[0]
    tok_dev = tv.shape[1]
    slots = experts * bucket
    first = (me * tok_dev).astype(F32)
    col = lax.broadcasted_iota(jnp.int32, (bucket, cap), 1).astype(F32)
    row = lax.broadcasted_iota(jnp.int32, (bucket, cap), 0).astype(F32)
    tok_at = lax.broadcasted_iota(jnp.int32, (bucket, tok_dev), 1).astype(F32)
    load_chosen.wait()
    picks = chosen[...].astype(F32)
    starts = jnp.sum(jnp.where(picks < first, 1.0, 0.0), axis=1, keepdims=True)
    ahead = picks + 1.0
    for k in range(experts):
        match = col == row + starts[k:k + 1, :]
        held = jnp.sum(jnp.where(match, ahead[k:k + 1, :], 0.0), axis=1, keepdims=True) - 1.0 - first
        hot[k * bucket:(k + 1) * bucket, :] = jnp.where(tok_at == held, 1.0, 0.0).astype(BF)

    for a in range(2):
        loads[a].wait()
        for k in range(2):
            packed = mm(hot[...], tv[a, :, k * share:(k + 1) * share], ((1,), (0,))).astype(BF)
            sx[a, :, k] = packed.reshape(slots // bucket, bucket, share)
        if a == 0:
            pl.semaphore_wait(barrier, ne + nt - 2)

        @pl.loop(1, ne)
        def _(d):
            to = (me + d) % ne
            rcopy(sx.at[a, to // 2, to % 2], rx.at[a, me], p1s.at[a, to], p1r.at[a, me], (to, t)).start()

        rx[a, me] = sx[a, me // 2, h]

    home_row = lax.broadcasted_iota(jnp.int32, (ne, cap), 0).astype(F32)
    place = lax.broadcasted_iota(jnp.int32, (ne, cap), 1).astype(F32)
    mine_row = jnp.sum(
        jnp.where(lax.broadcasted_iota(jnp.int32, (experts, cap), 0) == me // 2, chosen[...], 0).astype(F32),
        axis=0, keepdims=True,
    )
    low_bound = home_row * float(tok_dev)
    before = jnp.sum(jnp.where(mine_row < low_bound, 1.0, 0.0), axis=1, keepdims=True)
    inside = jnp.logical_and(mine_row >= low_bound, mine_row < low_bound + float(tok_dev))
    q = jnp.sum(jnp.where(inside, home_row * float(bucket) + place - before, 0.0), axis=0, keepdims=True)
    q_row[...] = jnp.broadcast_to(q, q_row.shape)
    q_col[...] = jnp.transpose(jnp.broadcast_to(q, (128, cap)))
    load_router.wait()
    router_all = rt[...].astype(F32)
    rrow[...] = jnp.broadcast_to(
        jnp.sum(
            jnp.where(lax.broadcasted_iota(jnp.int32, router_all.shape, 0) == me // 2, router_all, 0.0),
            axis=0, keepdims=True,
        ),
        rrow.shape,
    )

    own_g = 4 * y + 2 * c + h

    cut = (half + quarter // 2, half)

    def part_rows(a, part):
        return pl.ds(part * cut[a], cut[a] if part == 0 else cap - cut[a])

    def fan(a, y_, h_, target, part=None):
        g = 4 * y_ + 2 * c + h_
        j = 2 * y_ + h_
        dev = (zdev, ynd, ypd, cdev)[target]
        if part is None:
            ref = gx.at[a, g]
            send(ref, ref, ags.at[a, j, 0, target], agr.at[a, g, 0], dev)
        else:
            ref = gx.at[a, g, part_rows(a, part)]
            send(ref, ref, ags.at[a, j, part, target], agr.at[a, g, part], dev)

    def got(a, y_, h_):
        g = 4 * y_ + 2 * c + h_
        arrived(gx.at[a, g], agr.at[a, g, 0])

    def got_halves(a, y_, h_):
        g = 4 * y_ + 2 * c + h_
        for part in range(2):
            arrived(gx.at[a, g, part_rows(a, part)], agr.at[a, g, part])

    Z, N, B, C = 0, 1, 2, 3
    rows = 128

    buckets = ne * bucket
    def dispatched(a):
        @pl.loop(1, ne)
        def _(d):
            source = (me + ne - d) % ne
            arrived(rx.at[a, source], p1r.at[a, source])

    def compact(a):
        @pl.loop(0, cap // rows)
        def _(i):
            at = pl.ds(pl.multiple_of(i * rows, rows), rows)
            slot = lax.broadcasted_iota(jnp.int32, (rows, buckets), 1).astype(F32)
            pick = jnp.where(slot == q_col[at, 0:1], 1.0, 0.0).astype(BF)
            gx[a, own_g, at] = mm(pick, rx[a].reshape(buckets, share), ((1,), (0,))).astype(BF)

    acc[...] = jnp.zeros_like(acc)
    gp[...] = jnp.zeros_like(gp)

    def block_at(g):
        return pl.ds(pl.multiple_of(g * share, share), share)

    def add_x(g):
        x = gx[0, g]
        acc[0] += mm(x, w1v[block_at(g), :], ((1,), (0,)))
        gp[...] += x.astype(F32) * rrow[0:1, block_at(g)]

    def add_y(g):
        acc[1] += mm(gx[1, g], w2v[:, block_at(g)], ((1,), (1,)))

    def use(a, y_):
        @pl.loop(0, 2)
        def _(k):
            g = 4 * y_ + 2 * c + k
            o = 4 * y_ + 2 * (1 - c) + k
            (add_x, add_y)[a](g)
            arrived(gx.at[a, o], agr.at[a, o, 0])
            (add_x, add_y)[a](o)

    def got_half(a, y_, h_, part):
        g = 4 * y_ + 2 * c + h_
        arrived(gx.at[a, g, part_rows(a, part)], agr.at[a, g, part])

    def piece(a, y_, h_, part, k):
        g = 4 * y_ + 2 * c + h_
        whole = part_rows(a, part)
        return gx.at[a, g, pl.ds(whole.start + k * (whole.size // 2), whole.size // 2)]

    def relay(y_, h_, part, k, target):
        ref = piece(0, y_, h_, part, k)
        send(ref, ref, pcs.at[h_, part, k], pcr.at[h_, part, k], (zdev, ynd, ypd, cdev)[target])

    def got_pieces(y_, h_, part):
        for k in range(2):
            arrived(piece(0, y_, h_, part, k), pcr.at[h_, part, k])

    dispatched(0)
    compact(0)
    fan(0, y, h, N, 1)
    fan(0, y, h, B, 1)
    fan(0, y, h, N, 0)
    fan(0, y, h, B, 0)
    fan(0, y, h, Z, 1)
    fan(0, y, h, Z, 0)
    fan(0, y, h, C)
    for part in (1, 0):
        got_half(0, yp, h, part)
        relay(yp, h, part, 0, N)
        got_half(0, yn, h, part)
        relay(yn, h, part, 1, B)
    fan(0, yp, h, C)
    fan(0, yn, h, C)
    dispatched(1)
    compact(1)
    fan(1, y, h, Z)
    fan(1, y, h, N)
    fan(1, y, h, B)
    fan(1, y, h, C)
    fan(0, yp, h, Z, 0)
    fan(0, yn, h, Z, 0)
    got_pieces(yo, h, 0)
    fan(0, yo, h, Z, 0)
    got_pieces(yo, h, 1)
    fan(0, yo, h, C)
    loads[2].wait()
    got_half(0, y, 1 - h, 1)
    fan(0, y, 1 - h, N, 1)
    fan(0, y, 1 - h, B, 1)
    got_half(0, y, 1 - h, 0)
    fan(0, y, 1 - h, C)
    use(0, y)
    got(1, yp, h)
    fan(1, yp, h, N, 0)
    fan(1, yp, h, C)
    got(1, yn, h)
    fan(1, yn, h, B, 1)
    fan(1, yn, h, C)
    got(1, y, 1 - h)
    fan(1, y, 1 - h, N)
    fan(1, y, 1 - h, B)
    fan(1, y, 1 - h, C)
    loads[3].wait()
    got_half(0, yp, 1 - h, 1)
    relay(yp, 1 - h, 1, 0, N)
    got_half(0, yn, 1 - h, 1)
    relay(yn, 1 - h, 1, 1, B)
    use(1, y)
    got_halves(1, yo, h)
    fan(1, yo, h, C)
    got_half(0, yp, 1 - h, 0)
    fan(0, yp, 1 - h, C)
    got_half(0, yn, 1 - h, 0)
    fan(0, yn, 1 - h, C)
    use(0, yp)
    got(1, yp, 1 - h)
    fan(1, yp, 1 - h, N, 0)
    fan(1, yp, 1 - h, C)
    got(1, yn, 1 - h)
    fan(1, yn, 1 - h, B, 1)
    fan(1, yn, 1 - h, C)
    use(0, yn)
    got_half(0, yo, 1 - h, 0)
    got_pieces(yo, 1 - h, 1)
    fan(0, yo, 1 - h, C)
    use(1, yp)
    use(0, yo)
    use(1, yn)
    got_halves(1, yo, 1 - h)
    fan(1, yo, 1 - h, C)
    use(1, yo)

    er_rows = 64

    @pl.loop(0, cap // er_rows)
    def _(i):
        at = pl.ds(pl.multiple_of(i * er_rows, er_rows), er_rows)
        gate = jax.nn.sigmoid(jnp.sum(gp[at, :], axis=1, keepdims=True))
        pre = acc[0, at, :]
        up = acc[1, at, :]
        sig = jax.nn.sigmoid(pre)
        hidden = pre * sig
        hg[at, :] = (gate * hidden).astype(BF)
        gate_grad = jnp.sum(hidden * up, axis=1, keepdims=True)
        da[at, :] = (gate * up * sig * (1.0 + pre * (1.0 - sig))).astype(BF)
        score = gate_grad * gate * (1.0 - gate)
        dsb[at, :] = jnp.broadcast_to(score, (er_rows, dsb.shape[1]))

    def r_value(g):
        s = dsb[...]
        wide = jnp.concatenate([s, s], axis=1)
        return mm(da[...], w1v[block_at(g), :], ((1,), (1,))) + wide * rrow[0:1, block_at(g)]

    low = pl.ds(0, half)
    high = pl.ds(half, half)

    def partner(place_y):
        @pl.loop(0, 2)
        def _(k):
            i = 2 * place_y + k
            rb[i] = r_value(4 * place_y + 2 * (1 - c) + k).astype(BF)
            rcopy(rb.at[i], cb.at[i], cs.at[i], cr.at[i], cdev).start()

    def sums(place_y):
        @pl.loop(0, 2)
        def _(k):
            j = 2 * place_y + k
            value = r_value(4 * place_y + 2 * c + k)
            arrived(cb.at[j], cr.at[j])
            cb[j] = (cb[j].astype(F32) + value).astype(BF)

        send(cb.at[2 * place_y + 1 - h, low], zb.at[place_y], zzs.at[place_y], zzr.at[place_y], zdev)

    partner(yo)
    partner(yp)
    sums(yo)
    for k in range(2):
        send(cb.at[2 * yo + k, pl.ds(half, quarter)], yi.at[k, 0], yis.at[k, 0], yir.at[k, 0], ynd)
        send(cb.at[2 * yo + k, pl.ds(half + quarter, quarter)], yi.at[k, 1], yis.at[k, 1], yir.at[k, 1], ypd)
    partner(yn)
    sums(yp)
    partner(y)
    sums(yn)
    sums(y)

    def add_z(k):
        arrived(zb.at[k], zzr.at[k])
        zb[k] = (zb[k].astype(F32) + cb[2 * k + h, low].astype(F32)).astype(BF)

    add_z(yo)
    send(zb.at[yo, pl.ds(0, quarter)], yk.at[0], yks.at[0], ykr.at[0], ynd)
    send(zb.at[yo, pl.ds(quarter, quarter)], yk.at[1], yks.at[1], ykr.at[1], ypd)
    for k in range(2):
        arrived(yi.at[k, 0], yir.at[k, 0])
        arrived(yi.at[k, 1], yir.at[k, 1])
        first = pl.ds(half, quarter)
        second = pl.ds(half + quarter, quarter)
        cb[2 * yn + k, first] = (cb[2 * yn + k, first].astype(F32) + yi[k, 0].astype(F32)).astype(BF)
        cb[2 * yp + k, second] = (cb[2 * yp + k, second].astype(F32) + yi[k, 1].astype(F32)).astype(BF)
        send(cb.at[2 * yn + k, high], yj.at[k, 0], yjs.at[k, 0], yjr.at[k, 0], ynd)
        send(cb.at[2 * yp + k, high], yj.at[k, 1], yjs.at[k, 1], yjr.at[k, 1], ypd)

    s = dsb[...]
    s_hi = s.astype(BF).astype(F32)
    s_mid = (s - s_hi).astype(BF).astype(F32)
    s_lo = s - s_hi - s_mid
    lane = lax.broadcasted_iota(jnp.int32, s.shape, 1)
    terms = jnp.where(lane == 0, s_hi, jnp.where(lane == 1, s_mid, jnp.where(lane == 2, s_lo, 0.0)))
    terms = jnp.transpose(terms)[:16].astype(BF)

    @pl.loop(0, groups)
    def _(g):
        rp[g // 2, g % 2] = mm(terms, gx[0, g], ((1,), (0,)))[:8]

    @pl.loop(1, nt)
    def _(d):
        to = (t + d) % nt
        rcopy(rp.at[to], rq.at[t], r1s.at[to], r1r.at[t], (me, to)).start()

    def weight_grads(first, count):
        @pl.loop(first, first + count)
        def _(g):
            goutv[:, block_at(g)] = mm(hg[...], gx[1, g], ((0,), (0,))).astype(BF)
            ginv[block_at(g), :] = mm(gx[0, g], da[...], ((0,), (0,))).astype(BF)

    @pl.loop(1, nt)
    def _(d):
        source = (t + nt - d) % nt
        arrived(rq.at[source], r1r.at[source])

    rq[t] = rp[t]
    total = rq[0]
    for k in range(1, nt):
        total = total + rq[k]
    rs1[...] = total
    send(rs1.at[1 - h], rz, rzs, rzr, zdev)

    weight_grads(0, 4)
    add_z(yp)
    add_z(yn)
    first = pl.ds(0, quarter)
    second = pl.ds(quarter, quarter)
    for k in range(2):
        arrived(yk.at[k], ykr.at[k])
    zb[yn, first] = (zb[yn, first].astype(F32) + yk[0].astype(F32)).astype(BF)
    zb[yp, second] = (zb[yp, second].astype(F32) + yk[1].astype(F32)).astype(BF)
    send(zb.at[yn], yl.at[0], yls.at[0], ylr.at[0], ynd)
    send(zb.at[yp], yl.at[1], yls.at[1], ylr.at[1], ypd)
    base = 2 * y + 1 - h
    for k in range(2):
        for n in range(2):
            arrived(yj.at[k, n], yjr.at[k, n])
    cb[base, high] = (
        cb[base, high].astype(F32) + (yj[1 - h, 0].astype(F32) + yj[1 - h, 1].astype(F32))
    ).astype(BF)
    send(cb.at[base, high], zf, zfs, zfr, zdev)

    weight_grads(4, 6)

    mine = 2 * y + h
    arrived(zb.at[y], zzr.at[y])
    arrived(zf, zfr)
    fb[high, :] = (
        cb[mine, high].astype(F32) + (yj[h, 0].astype(F32) + yj[h, 1].astype(F32)) + zf[...].astype(F32)
    ).astype(BF)
    for side in range(2):
        arrived(yl.at[side], ylr.at[side])
    fb[low, :] = (
        cb[mine, low].astype(F32) + zb[y].astype(F32) + (yl[0].astype(F32) + yl[1].astype(F32))
    ).astype(BF)

    arrived(rz, rzr)
    router_sum = jnp.sum(rs1[h] + rz[...], axis=0, keepdims=True)
    rv[...] = jnp.broadcast_to(router_sum, rv.shape)
    rw[me] = jnp.broadcast_to(router_sum, rv.shape)

    @pl.loop(1, ne)
    def _(d):
        to = (me + d) % ne
        rcopy(rv, rw.at[me], r2s.at[to], r2r.at[me], (to, t)).start()

    homes = rows // bucket

    @pl.loop(0, ne // homes)
    def _(i):
        chunk = (i + me // homes) % (ne // homes)
        spread = (
            (lax.broadcasted_iota(jnp.int32, (rows, cap), 0) + chunk * rows).astype(F32) == q_row[0:1, :]
        ).astype(BF)
        es[pl.ds(chunk * homes, homes)] = (
            mm(spread, fb[...], ((1,), (0,))).astype(BF).reshape(homes, bucket, share)
        )

        @pl.loop(0, homes)
        def _(k):
            to = chunk * homes + (me + k) % homes

            @pl.when(to != me)
            def _():
                rcopy(es.at[to], er.at[me // 2, h], rets.at[to], retr.at[me], (to, t)).start()

    er[me // 2, h] = es[me]

    weight_grads(10, 6)
    out_copies = [
        pltpu.make_async_copy(ginv, gin, outs.at[0]),
        pltpu.make_async_copy(goutv, gout, outs.at[1]),
    ]
    for copy in out_copies:
        copy.start()

    @pl.loop(1, ne)
    def _(d):
        source = (me + ne - d) % ne
        arrived(rw.at[source], r2r.at[source])

    for k in range(ne):
        rxs[k // 2:k // 2 + 1, (k % 2) * share:(k % 2 + 1) * share] = rw[k, 0:1, :]
    ry[t] = rxs[...]

    @pl.loop(1, nt)
    def _(d):
        to = (t + d) % nt
        rcopy(rxs, ry.at[t], r3s.at[to], r3r.at[t], (me, to)).start()

    @pl.loop(1, nt)
    def _(d):
        source = (t + nt - d) % nt
        arrived(ry.at[source], r3r.at[source])

    for k in range(nt):
        gr[:, k * feat:(k + 1) * feat] = ry[k]

    @pl.loop(1, ne)
    def _(d):
        source = (me + ne - d) % ne
        arrived(er.at[source // 2, source % 2], retr.at[source])

    for k in range(2):
        gt[:, k * share:(k + 1) * share] = mm(hot[...], er[:, k].reshape(slots, share), ((0,), (0,))).astype(BF)

    @pl.loop(1, ne)
    def _(d):
        to = (me + d) % ne
        for a in range(2):
            rcopy(sx.at[a, 0, 0], rx.at[a, 0], p1s.at[a, to], p1r.at[a, to], zdev).wait_send()
        rcopy(rv, rw.at[0], r2s.at[to], r2r.at[to], zdev).wait_send()
        rcopy(es.at[0], er.at[0, 0], rets.at[to], retr.at[to], zdev).wait_send()

    @pl.loop(1, nt)
    def _(d):
        to = (t + d) % nt
        rcopy(rp.at[0], rq.at[0], r1s.at[to], r1r.at[to], zdev).wait_send()
        rcopy(rxs, ry.at[0], r3s.at[to], r3r.at[to], zdev).wait_send()

    @pl.loop(0, groups // 2)
    def _(j):
        rcopy(rb.at[j], cb.at[j], cs.at[j], cr.at[j], zdev).wait_send()

    for copy in pending:
        copy.wait_send()
    for copy in out_copies:
        copy.wait()


def hand_kernel(*refs):
    ins, outs, bufs = refs[:4], refs[4:8], refs[8:12]
    sin, sout = refs[12], refs[13]
    copies = []
    for n, (src, buf, dst) in enumerate(zip(ins, bufs, outs)):
        parts = 4 if src.shape[0] * src.shape[1] >= 1 << 19 else 1
        step = src.shape[0] // parts
        for k in range(parts):
            at = pl.ds(k * step, step)
            there = pltpu.make_async_copy(src.at[at], buf.at[at], sin.at[n, k])
            back = pltpu.make_async_copy(buf.at[at], dst.at[at], sout.at[n, k])
            there.start()
            copies.append((there, back))
    for there, back in copies:
        there.wait()
        back.start()
    for _, back in copies:
        back.wait()


def hand_out(*arrays):
    aspec = pl.BlockSpec(memory_space=pl.ANY)
    return pl.pallas_call(
        hand_kernel,
        out_shape=tuple(jax.ShapeDtypeStruct(v.shape, v.dtype) for v in arrays),
        in_specs=[aspec] * 4,
        out_specs=(aspec,) * 4,
        scratch_shapes=[pltpu.VMEM(v.shape, v.dtype) for v in arrays]
        + [pltpu.SemaphoreType.DMA((4, 4)), pltpu.SemaphoreType.DMA((4, 4))],
        name="hand_out",
    )(*arrays)


def body(tokens, cotangent, w_in, w_out, router, chosen):
    tok_dev, features = tokens.shape
    hidden = w_in.shape[1]
    ne = lax.axis_size("expert")
    nt = lax.axis_size("tensor")
    bucket = 4 * tok_dev // ne
    experts, cap = chosen.shape
    feat = features // nt
    share = feat // 2
    groups = features // share

    vm = lambda shape, kind: pltpu.VMEM(shape, kind)
    dma = lambda *shape: pltpu.SemaphoreType.DMA(shape)
    vspec = pl.BlockSpec(memory_space=pltpu.VMEM)
    aspec = pl.BlockSpec(memory_space=pl.ANY)
    half, quarter = cap // 2, cap // 4
    g2 = groups // 2
    scratch = [
        vm((experts, cap), jnp.int32),
        vm((experts, features), BF),
        vm((8, features), F32),
        vm((experts * bucket, tok_dev), BF),
        vm((8, cap), F32),
        vm((cap, 128), F32),
        vm((2, tok_dev, feat), BF),
        vm((features, hidden), BF),
        vm((hidden, features), BF),
        vm((2, experts, 2, bucket, share), BF),
        vm((2, ne, bucket, share), BF),
        vm((2, groups, cap, share), BF),
        vm((2, cap, hidden), F32),
        vm((cap, share), F32),
        vm((cap, hidden), BF),
        vm((cap, hidden), BF),
        vm((cap, 128), F32),
        vm((g2, cap, share), BF),
        vm((g2, cap, share), BF),
        vm((RING, half, share), BF),
        vm((2, 2, quarter, share), BF),
        vm((2, 2, half, share), BF),
        vm((2, quarter, share), BF),
        vm((2, half, share), BF),
        vm((half, share), BF),
        vm((8, 128), F32),
        vm((cap, share), BF),
        vm((ne, bucket, share), BF),
        vm((experts, 2, bucket, share), BF),
        vm((features, hidden), BF),
        vm((hidden, features), BF),
        vm((nt, 2, 8, share), F32),
        vm((nt, 2, 8, share), F32),
        vm((2, 8, share), F32),
        vm((8, share), F32),
        vm((8, share), F32),
        vm((ne, 8, share), F32),
        vm((experts, feat), F32),
        vm((nt, experts, feat), F32),
        dma(6), dma(2, ne), dma(2, ne), dma(2, 2, 2), dma(2, 2, 2), dma(2, g2, 2, 4), dma(2, groups, 2),
        dma(g2), dma(g2), dma(RING), dma(RING), dma(2, 2), dma(2, 2), dma(2, 2), dma(2, 2),
        dma(2), dma(2), dma(2), dma(2), pltpu.SemaphoreType.DMA, pltpu.SemaphoreType.DMA,
        dma(ne), dma(ne), dma(nt), dma(nt), pltpu.SemaphoreType.DMA, pltpu.SemaphoreType.DMA,
        dma(ne), dma(ne), dma(nt), dma(nt), dma(2),
    ]
    gt, gin, gout, gr = pl.pallas_call(
        functools.partial(step_kernel, ne, nt, bucket),
        out_shape=(
            jax.ShapeDtypeStruct((tok_dev, feat), BF),
            jax.ShapeDtypeStruct((features, hidden), BF),
            jax.ShapeDtypeStruct((hidden, features), BF),
            jax.ShapeDtypeStruct((experts, features), F32),
        ),
        in_specs=[aspec] * 6,
        out_specs=(vspec, aspec, aspec, vspec),
        scratch_shapes=scratch,
        compiler_params=pltpu.CompilerParams(
            collective_id=0, has_side_effects=True, vmem_limit_bytes=60 * 1024 * 1024
        ),
        name="moe_step",
    )(
        tokens, cotangent, w_in, w_out, router.T, chosen,
    )
    gt, gin, gout, gr = hand_out(gt, gin, gout, gr)
    return gt, gin, gout, gr.T


def solution(mesh):
    placed = (
        P("expert", None),
        P("expert", None),
        P(None, ("expert", "tensor")),
        P(("expert", "tensor"), None),
        P(),
        P(),
    )
    return jax.shard_map(
        body,
        mesh=mesh,
        in_specs=placed,
        out_specs=(
            P("expert", "tensor"),
            P(None, ("expert", "tensor")),
            P(("expert", "tensor"), None),
            P(),
        ),
        check_vma=False,
    )
```

time: 137 us -> 119 us (0.87)
  local copies, waits for them, and re-layouts: 10.9 us -> 0 us
  other arithmetic: 4.86 us -> 0 us
  Pallas kernels: 121 us -> 118 us
    pallas_call x1, Pallas kernels: 121 us -> 114 us  [body(): pl.pallas_call(functools.partial(step_kernel, ne, nt, bucket), out_shape=...]
    unnamed x8 -> x0, local copies, waits for them, and re-layouts: 6.89 us -> none
    pallas_call x0 -> x1, Pallas kernels: none -> 4.3 us  [hand_out(): pl.pallas_call(hand_kernel, out_shape=tuple((jax.ShapeDtypeStruct(v.shape...]
    sub x3 -> x0, other arithmetic: 2.2 us -> none  [the longest x2 2.19 us: body(): q = home * bucket + place - before]
    reduce_sum x3 -> x0, other arithmetic: 1.68 us -> none  [the longest x1 0.87 us: body(): starts = jnp.sum((chosen < first).astype(jnp.int32), axis=1)]
    sub x2 -> x0, local copies, waits for them, and re-layouts: 1.62 us -> none  [body(): jnp.sum(jnp.where(place[None, None, :] == want[:, :, None], chosen[:, Non...]
where the time goes in v3:
time: 119 us
  Pallas kernels  118 us (99%)
    pallas_call x1, Pallas kernels, body(): pl.pallas_call(functools.partial(step_kernel, ne, nt, bucket), out_shape=...  114 us
    pallas_call x1, Pallas kernels, hand_out(): pl.pallas_call(hand_kernel, out_shape=tuple((jax.ShapeDtypeStruct(v.shape...  4.3 us

profile of v3, /device:TPU:1, one launch (start us, length us, event | category | flops | bytes accessed | tf_op | source)
XLA Modules:
  0.0 118.6 jit_solution(6275287648717842288)
XLA Ops:
  0.6 113.7 %moe_step.1 = (bf16[256,512]{1,0:T(8,128)(2,1)}, bf16[4096,256]{1,0:T(8,128)(2,1)}, bf16[256,4096]{1,0:T(8,128)(2,1)}, f32[16,4096]{1,0:T(8,128)}) custom-call(bf16[256,4096]{1,0:T(8,128)(2,1)} %tok.1, bf16[256,4096]{1,0:T(8,128)(2,1)} %cot.1, bf16[4096,256]{1,0:T(8,128)(2,1)} %w_in.1, bf16[256,4096]{1,0:T(8,128)(2,1)} %w_out.1, bf16[16,4096]{1,0:T(8,128)(2,1)} %bitcast.2, ...), custom_call_target="tpu_custom_call" | custom-call | tf_op jit(solution)/shard_map/moe_step/pallas_call | solution.py:632
  114.3 4.3 %hand_out.1 = (bf16[256,512]{1,0:T(8,128)(2,1)}, bf16[4096,256]{1,0:T(8,128)(2,1)}, bf16[256,4096]{1,0:T(8,128)(2,1)}, f32[16,4096]{1,0:T(8,128)}) custom-call(bf16[256,512]{1,0:T(8,128)(2,1)} %get-tuple-element.12.refs_0_, bf16[4096,256]{1,0:T(8,128)(2,1)} %get-tuple-element.13.refs_1_, bf16[256,4096]{1,0:T(8,128)(2,1)} %get-tuple-element.14.refs_2_, ...), custom_call_target="tpu_custom_call" | custom-call | tf_op jit(solution)/shard_map/hand_out/pallas_call | solution.py:558

commit v4 on v3

--- a/solution.py
+++ b/solution.py
@@ -21,11 +21,11 @@
     ne, nt, bucket,
     tok, cot, w_in, w_out, rt_any, chosen_any,
     gt, gin, gout, gr,
-    chosen, rt, rrow, hot, q_row, q_col,
+    chosen, rt, rrow, hot, hot_t, gather, spread, q_col,
     tv, w1v, w2v, sx, rx, gx, acc, gp, hg, da, dsb, rb, cb, zb, yi, yj, yk, yl, zf, fv, fb, es, er,
-    ginv, goutv, rp, rq, rs1, rz, rv, rw, rxs, ry,
+    rp, rq, rs1, rz, rv, rw, rxs, ry,
     ld, p1s, p1r, pcs, pcr, ags, agr, cs, cr, zzs, zzr, yis, yir, yjs, yjr, yks, ykr, yls, ylr, zfs, zfr,
-    rets, retr, r1s, r1r, rzs, rzr, r2s, r2r, r3s, r3r, outs,
+    rets, retr, r1s, r1r, rzs, rzr, r2s, r2r, r3s, r3r,
 ):
     me = lax.axis_index("expert")
     t = lax.axis_index("tensor")
@@ -128,7 +128,6 @@
     before = jnp.sum(jnp.where(mine_row < low_bound, 1.0, 0.0), axis=1, keepdims=True)
     inside = jnp.logical_and(mine_row >= low_bound, mine_row < low_bound + float(tok_dev))
     q = jnp.sum(jnp.where(inside, home_row * float(bucket) + place - before, 0.0), axis=0, keepdims=True)
-    q_row[...] = jnp.broadcast_to(q, q_row.shape)
     q_col[...] = jnp.transpose(jnp.broadcast_to(q, (128, cap)))
     load_router.wait()
     router_all = rt[...].astype(F32)
@@ -140,6 +139,21 @@
         rrow.shape,
     )
 
+    hot_t[...] = jnp.transpose(hot[...].astype(F32)).astype(BF)
+    rows = 128
+
+    @pl.loop(0, cap // rows)
+    def _(i):
+        at = pl.ds(pl.multiple_of(i * rows, rows), rows)
+        slot = lax.broadcasted_iota(jnp.int32, (rows, ne * bucket), 1).astype(F32)
+        gather[at, :] = jnp.where(slot == q_col[at, 0:1], 1.0, 0.0).astype(BF)
+
+    @pl.loop(0, ne * bucket // rows)
+    def _(i):
+        at = pl.ds(pl.multiple_of(i * rows, rows), rows)
+        slot = (lax.broadcasted_iota(jnp.int32, (rows, cap), 0) + i * rows).astype(F32)
+        spread[at, :] = jnp.where(slot == q, 1.0, 0.0).astype(BF)
+
     own_g = 4 * y + 2 * c + h
 
     cut = (half + quarter // 2, half)
@@ -168,7 +182,6 @@
             arrived(gx.at[a, g, part_rows(a, part)], agr.at[a, g, part])
 
     Z, N, B, C = 0, 1, 2, 3
-    rows = 128
 
     buckets = ne * bucket
     def dispatched(a):
@@ -181,9 +194,7 @@
         @pl.loop(0, cap // rows)
         def _(i):
             at = pl.ds(pl.multiple_of(i * rows, rows), rows)
-            slot = lax.broadcasted_iota(jnp.int32, (rows, buckets), 1).astype(F32)
-            pick = jnp.where(slot == q_col[at, 0:1], 1.0, 0.0).astype(BF)
-            gx[a, own_g, at] = mm(pick, rx[a].reshape(buckets, share), ((1,), (0,))).astype(BF)
+            gx[a, own_g, at] = mm(gather[at, :], rx[a].reshape(buckets, share), ((1,), (0,))).astype(BF)
 
     acc[...] = jnp.zeros_like(acc)
     gp[...] = jnp.zeros_like(gp)
@@ -390,8 +401,8 @@
     def weight_grads(first, count):
         @pl.loop(first, first + count)
         def _(g):
-            goutv[:, block_at(g)] = mm(hg[...], gx[1, g], ((0,), (0,))).astype(BF)
-            ginv[block_at(g), :] = mm(gx[0, g], da[...], ((0,), (0,))).astype(BF)
+            gout[:, block_at(g)] = mm(hg[...], gx[1, g], ((0,), (0,))).astype(BF)
+            gin[block_at(g), :] = mm(gx[0, g], da[...], ((0,), (0,))).astype(BF)
 
     @pl.loop(1, nt)
     def _(d):
@@ -454,11 +465,9 @@
     @pl.loop(0, ne // homes)
     def _(i):
         chunk = (i + me // homes) % (ne // homes)
-        spread = (
-            (lax.broadcasted_iota(jnp.int32, (rows, cap), 0) + chunk * rows).astype(F32) == q_row[0:1, :]
-        ).astype(BF)
+        at = pl.ds(pl.multiple_of(chunk * rows, rows), rows)
         es[pl.ds(chunk * homes, homes)] = (
-            mm(spread, fb[...], ((1,), (0,))).astype(BF).reshape(homes, bucket, share)
+            mm(spread[at, :], fb[...], ((1,), (0,))).astype(BF).reshape(homes, bucket, share)
         )
 
         @pl.loop(0, homes)
@@ -472,13 +481,6 @@
     er[me // 2, h] = es[me]
 
     weight_grads(10, 6)
-    out_copies = [
-        pltpu.make_async_copy(ginv, gin, outs.at[0]),
-        pltpu.make_async_copy(goutv, gout, outs.at[1]),
-    ]
-    for copy in out_copies:
-        copy.start()
-
     @pl.loop(1, ne)
     def _(d):
         source = (me + ne - d) % ne
@@ -507,7 +509,7 @@
         arrived(er.at[source // 2, source % 2], retr.at[source])
 
     for k in range(2):
-        gt[:, k * share:(k + 1) * share] = mm(hot[...], er[:, k].reshape(slots, share), ((0,), (0,))).astype(BF)
+        gt[:, k * share:(k + 1) * share] = mm(hot_t[...], er[:, k].reshape(slots, share), ((1,), (0,))).astype(BF)
 
     @pl.loop(1, ne)
     def _(d):
@@ -529,39 +531,27 @@
 
     for copy in pending:
         copy.wait_send()
-    for copy in out_copies:
+
+
+def hand_kernel(*refs):
+    ins, outs = refs[:4], refs[4:8]
+    copies = [pltpu.make_async_copy(a, b, refs[8].at[n]) for n, (a, b) in enumerate(zip(ins, outs))]
+    for copy in copies:
+        copy.start()
+    for copy in copies:
         copy.wait()
-
-
-def hand_kernel(*refs):
-    ins, outs, bufs = refs[:4], refs[4:8], refs[8:12]
-    sin, sout = refs[12], refs[13]
-    copies = []
-    for n, (src, buf, dst) in enumerate(zip(ins, bufs, outs)):
-        parts = 4 if src.shape[0] * src.shape[1] >= 1 << 19 else 1
-        step = src.shape[0] // parts
-        for k in range(parts):
-            at = pl.ds(k * step, step)
-            there = pltpu.make_async_copy(src.at[at], buf.at[at], sin.at[n, k])
-            back = pltpu.make_async_copy(buf.at[at], dst.at[at], sout.at[n, k])
-            there.start()
-            copies.append((there, back))
-    for there, back in copies:
-        there.wait()
-        back.start()
-    for _, back in copies:
-        back.wait()
 
 
 def hand_out(*arrays):
     aspec = pl.BlockSpec(memory_space=pl.ANY)
+    vspec = pl.BlockSpec(memory_space=pltpu.VMEM)
     return pl.pallas_call(
         hand_kernel,
         out_shape=tuple(jax.ShapeDtypeStruct(v.shape, v.dtype) for v in arrays),
-        in_specs=[aspec] * 4,
+        in_specs=[vspec] * 4,
         out_specs=(aspec,) * 4,
-        scratch_shapes=[pltpu.VMEM(v.shape, v.dtype) for v in arrays]
-        + [pltpu.SemaphoreType.DMA((4, 4)), pltpu.SemaphoreType.DMA((4, 4))],
+        scratch_shapes=[pltpu.SemaphoreType.DMA((4,))],
+        compiler_params=pltpu.CompilerParams(vmem_limit_bytes=16 * 1024 * 1024),
         name="hand_out",
     )(*arrays)
 
@@ -588,7 +578,9 @@
         vm((experts, features), BF),
         vm((8, features), F32),
         vm((experts * bucket, tok_dev), BF),
-        vm((8, cap), F32),
+        vm((tok_dev, experts * bucket), BF),
+        vm((cap, ne * bucket), BF),
+        vm((ne * bucket, cap), BF),
         vm((cap, 128), F32),
         vm((2, tok_dev, feat), BF),
         vm((features, hidden), BF),
@@ -613,8 +605,6 @@
         vm((cap, share), BF),
         vm((ne, bucket, share), BF),
         vm((experts, 2, bucket, share), BF),
-        vm((features, hidden), BF),
-        vm((hidden, features), BF),
         vm((nt, 2, 8, share), F32),
         vm((nt, 2, 8, share), F32),
         vm((2, 8, share), F32),
@@ -627,7 +617,7 @@
         dma(g2), dma(g2), dma(RING), dma(RING), dma(2, 2), dma(2, 2), dma(2, 2), dma(2, 2),
         dma(2), dma(2), dma(2), dma(2), pltpu.SemaphoreType.DMA, pltpu.SemaphoreType.DMA,
         dma(ne), dma(ne), dma(nt), dma(nt), pltpu.SemaphoreType.DMA, pltpu.SemaphoreType.DMA,
-        dma(ne), dma(ne), dma(nt), dma(nt), dma(2),
+        dma(ne), dma(ne), dma(nt), dma(nt),
     ]
     gt, gin, gout, gr = pl.pallas_call(
         functools.partial(step_kernel, ne, nt, bucket),
@@ -637,11 +627,11 @@
             jax.ShapeDtypeStruct((hidden, features), BF),
             jax.ShapeDtypeStruct((experts, features), F32),
         ),
-        in_specs=[aspec] * 6,
-        out_specs=(vspec, aspec, aspec, vspec),
+        in_specs=[pl.BlockSpec(memory_space=pltpu.HBM)] * 6,
+        out_specs=(vspec,) * 4,
         scratch_shapes=scratch,
         compiler_params=pltpu.CompilerParams(
-            collective_id=0, has_side_effects=True, vmem_limit_bytes=60 * 1024 * 1024
+            collective_id=0, has_side_effects=True, vmem_limit_bytes=48 * 1024 * 1024
         ),
         name="moe_step",
     )(

time: 119 us -> 117 us (0.983)
  Pallas kernels: 118 us -> 115 us
  local copies, waits for them, and re-layouts: 0 us -> 1.65 us
    pallas_call x1, Pallas kernels: 4.3 us -> 2.21 us  [hand_out(): pl.pallas_call(hand_kernel, out_shape=tuple((jax.ShapeDtypeStruct(v.shape...]
    unnamed x0 -> x4, local copies, waits for them, and re-layouts: none -> 1.65 us
    pallas_call x1, Pallas kernels: 114 us -> 112 us  [body(): pl.pallas_call(functools.partial(step_kernel, ne, nt, bucket), out_shape=...]
where the time goes in v4:
time: 117 us
  Pallas kernels  115 us (98%)
  local copies, waits for them, and re-layouts  1.65 us (1%)
    pallas_call x1, Pallas kernels, body(): pl.pallas_call(functools.partial(step_kernel, ne, nt, bucket), out_shape=...  112 us

profile of v4, /device:TPU:1, one launch (start us, length us, event | category | flops | bytes accessed | tf_op | source)
XLA Modules:
  0.0 117.0 jit_solution(3301832954517016927)
XLA Ops:
  0.6 0.0 copy-start
  0.6 0.9 copy-done
  1.5 0.0 copy-start.1
  1.5 0.8 copy-done.1
  2.3 112.5 %moe_step.1 = (bf16[256,512]{1,0:T(8,128)(2,1)S(1)}, bf16[4096,256]{1,0:T(8,128)(2,1)S(1)}, bf16[256,4096]{1,0:T(8,128)(2,1)S(1)}, f32[16,4096]{1,0:T(8,128)S(1)}) custom-call(bf16[256,4096]{1,0:T(8,128)(2,1)} %tok.1, bf16[256,4096]{1,0:T(8,128)(2,1)} %cot.1, bf16[4096,256]{1,0:T(8,128)(2,1)} %w_in.1, bf16[256,4096]{1,0:T(8,128)(2,1)} %w_out.1, ...), custom_call_target="tpu_custom_call" | custom-call | tf_op jit(solution)/shard_map/moe_step/pallas_call | solution.py:622
  114.8 2.2 %hand_out.1 = (bf16[256,512]{1,0:T(8,128)(2,1)}, bf16[4096,256]{1,0:T(8,128)(2,1)}, bf16[256,4096]{1,0:T(8,128)(2,1)}, f32[16,4096]{1,0:T(8,128)}) custom-call(bf16[256,512]{1,0:T(8,128)(2,1)S(1)} %get-tuple-element.12.refs_0_, bf16[4096,256]{1,0:T(8,128)(2,1)S(1)} %get-tuple-element.13.refs_1_, bf16[256,4096]{1,0:T(8,128)(2,1)S(1)} %get-tuple-element.14.refs_2_, ...), custom_call_target="tpu_custom_call" | custom-call | tf_op jit(solution)/shard_map/hand_out/pallas_call | solution.py:548
Async XLA Ops:
  0.6 0.9 copy-start
  1.5 0.8 copy-start.1

commit v5 on v4

--- a/solution.py
+++ b/solution.py
@@ -268,9 +268,6 @@
     got_half(0, y, 1 - h, 1)
     fan(0, y, 1 - h, N, 1)
     fan(0, y, 1 - h, B, 1)
-    got_half(0, y, 1 - h, 0)
-    fan(0, y, 1 - h, C)
-    use(0, y)
     got(1, yp, h)
     fan(1, yp, h, N, 0)
     fan(1, yp, h, C)
@@ -281,6 +278,9 @@
     fan(1, y, 1 - h, N)
     fan(1, y, 1 - h, B)
     fan(1, y, 1 - h, C)
+    got_half(0, y, 1 - h, 0)
+    fan(0, y, 1 - h, C)
+    use(0, y)
     loads[3].wait()
     got_half(0, yp, 1 - h, 1)
     relay(yp, 1 - h, 1, 0, N)
@@ -635,7 +635,9 @@
         ),
         name="moe_step",
     )(
-        tokens, cotangent, w_in, w_out, router.T, chosen,
+        tokens, cotangent, w_in, w_out,
+        pltpu.with_memory_space_constraint(router.T, pltpu.HBM),
+        pltpu.with_memory_space_constraint(chosen, pltpu.HBM),
     )
     gt, gin, gout, gr = hand_out(gt, gin, gout, gr)
     return gt, gin, gout, gr.T

time: 117 us -> 116 us (level)
  local copies, waits for them, and re-layouts: 1.65 us -> 0 us
    unnamed x4 -> x0, local copies, waits for them, and re-layouts: 1.65 us -> none
where the time goes in v5:
time: 116 us; the launch traced here: 115 us
  Pallas kernels  115 us (99%)
    pallas_call x1, Pallas kernels, body(): pl.pallas_call(functools.partial(step_kernel, ne, nt, bucket), out_shape=...  113 us

profile of v5, /device:TPU:1, one launch (start us, length us, event | category | flops | bytes accessed | tf_op | source)
XLA Modules:
  0.0 115.4 jit_solution(14357624076915686672)
XLA Ops:
  0.6 112.6 %moe_step.1 = (bf16[256,512]{1,0:T(8,128)(2,1)S(1)}, bf16[4096,256]{1,0:T(8,128)(2,1)S(1)}, bf16[256,4096]{1,0:T(8,128)(2,1)S(1)}, f32[16,4096]{1,0:T(8,128)S(1)}) custom-call(bf16[256,4096]{1,0:T(8,128)(2,1)} %tok.1, bf16[256,4096]{1,0:T(8,128)(2,1)} %cot.1, bf16[4096,256]{1,0:T(8,128)(2,1)} %w_in.1, bf16[256,4096]{1,0:T(8,128)(2,1)} %w_out.1, ...), custom_call_target="tpu_custom_call" | custom-call | tf_op jit(solution)/shard_map/moe_step/pallas_call | solution.py:622
  113.2 2.2 %hand_out.1 = (bf16[256,512]{1,0:T(8,128)(2,1)}, bf16[4096,256]{1,0:T(8,128)(2,1)}, bf16[256,4096]{1,0:T(8,128)(2,1)}, f32[16,4096]{1,0:T(8,128)}) custom-call(bf16[256,512]{1,0:T(8,128)(2,1)S(1)} %get-tuple-element.12.refs_0_, bf16[4096,256]{1,0:T(8,128)(2,1)S(1)} %get-tuple-element.13.refs_1_, bf16[256,4096]{1,0:T(8,128)(2,1)S(1)} %get-tuple-element.14.refs_2_, ...), custom_call_target="tpu_custom_call" | custom-call | tf_op jit(solution)/shard_map/hand_out/pallas_call | solution.py:548
